TPU v7x, 512 devices: a whole 4x4x16 slice. The times are simulated.
512 devices in a mesh: ctx: 32 (over y, x, core), hg: 16 (over z).
Axes of the slice: x: 4, y: 4, z: 16, core: 2. Of those that a mesh axis runs over, the one named last changes fastest.
Arguments:
- queries: bfloat16 [65536, 2048], P('ctx', 'hg'), may hold values from -17 to 17
- keys: bfloat16 [65536, 2048], P('ctx', 'hg'), may hold values from -10 to 10
- values: bfloat16 [65536, 2048], P('ctx', 'hg'), may hold values from -8 to 8
- cluster_ids: int32 [16, 65536, 1], P('hg', 'ctx'), may hold values from 0 to 511; in each aligned block of 2048 rows (0 to 2047, 2048 to 4095, ..., all dimensions but the last counted through in order) at most 8 rows name the same one
- w_out: bfloat16 [2048, 2048], P(None, 'hg'), may hold values from -0.125 to 0.125
- old_sums: float32 [16, 512, 128], P('hg', 'ctx'), may hold values from -24 to 24
Outputs:
- projected: bfloat16 [65536, 2048], P('ctx', 'hg')
- centroid_sums: float32 [16, 512, 128], P('hg', 'ctx')
Inputs may be any that keep to these rules, and one draw needn't show every extreme that they name: `cluster_ids`: for each head, the 2048 tokens of one index of ctx (aligned blocks along the token dimension) name no cluster more than 8 times, a bound that some block reaches.
All inputs are finite; a program needn't handle non-finite values.
Results may differ from a plain program's by a relative error of at most 0.015.
Values may be sent and summed in bfloat16 or wider, within the bound.
No kernel may reach another device: no remote copies, remote signals or barrier semaphores. Data moves between devices by JAX's collectives and lax.ppermute only.
A program may use at most 64 MiB of HBM per device.

v0:
```python
import jax
import jax.numpy as jnp
from jax import lax
from jax.sharding import PartitionSpec as P

HD = 128
NCL = 512
SLOTS = 8


DECAY = 0.9
NEG_FILL = -1e30


def on_device(queries, keys, values, cluster_ids, w_out, old_sums):
    ctx_count = lax.axis_size("ctx")
    local_count = NCL // ctx_count
    heads_dev = cluster_ids.shape[0]
    tok_rows = queries.shape[0]
    cluster_of = cluster_ids[:, :, 0]

    def split_heads(source):
        return source.reshape(tok_rows, heads_dev, HD).transpose(1, 0, 2)

    packed = jnp.concatenate([split_heads(queries), split_heads(keys), split_heads(values)], axis=2)
    position = jnp.arange(tok_rows, dtype=jnp.int32)

    def rank_one(head_ids):
        same_before = (head_ids[:, None] == head_ids[None, :]) & (
            position[None, :] < position[:, None]
        )
        return jnp.sum(same_before, axis=1, dtype=jnp.int32)

    slot_rank = lax.map(rank_one, cluster_of)
    target = cluster_of * SLOTS + slot_rank

    def place_rows(source, where_to):
        return jnp.zeros((NCL * SLOTS, source.shape[1]), source.dtype).at[where_to].set(source)

    outgoing = jax.vmap(place_rows)(packed, target).reshape(
        heads_dev, ctx_count, local_count, SLOTS, 3 * HD
    )
    live_flags = jax.vmap(place_rows)(jnp.ones((heads_dev, tok_rows, 1), jnp.bfloat16), target)
    live_flags = live_flags.reshape(heads_dev, ctx_count, local_count, SLOTS, 1)
    slab_rows = lax.all_to_all(outgoing, "ctx", split_axis=1, concat_axis=1, tiled=True)
    mark_rows = lax.all_to_all(live_flags, "ctx", split_axis=1, concat_axis=1, tiled=True)
    groups = slab_rows.shape[2]
    key_count = ctx_count * SLOTS
    slab_rows = slab_rows.transpose(0, 2, 1, 3, 4).reshape(heads_dev, groups, key_count, 3 * HD)
    mark_rows = mark_rows.transpose(0, 2, 1, 3, 4).reshape(heads_dev, groups, key_count)
    query_rows = slab_rows[..., :HD]
    key_rows = slab_rows[..., HD : 2 * HD]
    value_rows = slab_rows[..., 2 * HD :]
    scores = jnp.einsum(
        "hcqd,hckd->hcqk", query_rows, key_rows, preferred_element_type=jnp.float32
    ) * HD ** (-0.5)
    present = (mark_rows > 0)[:, :, None, :]
    scores = jnp.where(present, scores, NEG_FILL)
    row_max = jnp.max(scores, axis=3, keepdims=True)
    weights = jnp.exp(scores - row_max)
    probabilities = (weights / jnp.sum(weights, axis=3, keepdims=True)).astype(jnp.bfloat16)
    mixed_rows = jnp.einsum(
        "hcqk,hckd->hcqd", probabilities, value_rows, preferred_element_type=jnp.float32
    ).astype(jnp.bfloat16)
    mixed_rows = mixed_rows.reshape(heads_dev, groups, ctx_count, SLOTS, HD).transpose(
        0, 2, 1, 3, 4
    )
    result = mixed_rows
    mixed_rows = result
    returned = lax.all_to_all(mixed_rows, "ctx", split_axis=1, concat_axis=1, tiled=True)
    flat_back = returned.reshape(heads_dev, NCL * SLOTS, HD)
    attention = jnp.take_along_axis(flat_back, target[:, :, None], axis=1)
    attention = attention.transpose(1, 0, 2).reshape(tok_rows, heads_dev * HD)
    projected = jnp.dot(
        lax.all_gather(attention, "hg", axis=1, tiled=True),
        w_out,
        preferred_element_type=jnp.float32,
    ).astype(jnp.bfloat16)
    onehot = (cluster_of[:, :, None] == jnp.arange(NCL, dtype=jnp.int32)[None, None, :]).astype(
        jnp.bfloat16
    )
    partial_value = jnp.einsum(
        "htc,htd->hcd", onehot, packed[..., HD : 2 * HD], preferred_element_type=jnp.float32
    )
    member_sums = lax.psum_scatter(
        partial_value.astype(jnp.bfloat16), "ctx", scatter_dimension=1, tiled=True
    ).astype(jnp.float32)
    centroid_sums = DECAY * old_sums + (1.0 - DECAY) * member_sums
    return (projected, centroid_sums)


def solution(mesh):
    placed = (
        P("ctx", "hg"),
        P("ctx", "hg"),
        P("ctx", "hg"),
        P("hg", "ctx", None),
        P(None, "hg"),
        P("hg", "ctx", None),
    )
    return jax.shard_map(
        on_device,
        mesh=mesh,
        in_specs=placed,
        out_specs=(P("ctx", "hg"), P("hg", "ctx", None)),
        check_vma=False,
    )
```

profile of v0, /device:TPU:74, one launch (start us, length us, event | category | flops | bytes accessed | tf_op | source)
XLA Modules:
  0.0 280.2 jit_solution(8318779818847726390)
XLA Ops:
  8.0 0.0 copy-start
  8.0 5.2 %convert_reduce_fusion = s32[2048]{0:T(1024)S(1)} fusion(s32[2048]{0:T(1024)} %bitcast.47), kind=kLoop, calls=%fused_computation.4 | loop fusion | flops 20969472 | bytes 16384 | tf_op jit(solution)/shard_map/while/body/eval_jaxpr/reduce_sum | solution.py:32
  13.2 0.7 and_reduce_fusion.1
  14.0 0.7 fusion.20
  14.7 0.8 and_reduce_fusion
  15.5 14.6 %scatter_custom_fusion = bf16[4096]{0:T(1024)(128)(2,1)S(1)} fusion(s32[2048]{0:T(1024)S(1)} %broadcast_select_fusion.1, bf16[2048]{0:T(1024)(128)(2,1)S(1)} %broadcast.100, bf16[]{:T(256)} %constant.10.clone.1), kind=kCustom, calls=%fused_computation.45 | custom fusion | bytes 8194
  30.1 0.2 reshape.150
  30.3 0.7 copy.21
  31.0 7.5 %all-to-all-start = ((bf16[1,32,16,8,1]{2,3,4,0,1:T(8,128)(2,1)}), bf16[1,32,16,8,1]{2,3,4,0,1:T(8,128)(2,1)S(1)}, u32[]{:S(2)}, u32[]{:S(2)}) async-start(bf16[1,32,16,8,1]{2,3,4,0,1:T(8,128)(2,1)} %copy.21), calls=%async_computation | async-start | bytes 131072 | tf_op jit(solution)/shard_map/all_to_all | solution.py:46
  38.5 12.1 %scatter_custom_fusion.1 = bf16[4096,384]{1,0:T(8,128)(2,1)} fusion(s32[2048]{0:T(1024)S(1)} %broadcast_select_fusion.1, bf16[1,2048,128]{2,1,0:T(8,128)(2,1)} %bitcast.43, bf16[]{:T(256)} %constant.67, bf16[1,2048,128]{2,1,0:T(8,128)(2,1)} %bitcast.45, bf16[1,2048,128]{2,1,0:T(8,128)(2,1)} %bitcast.44, bf16[]{:T(256)} %constant.10.clone.1), kind=kCustom, calls=%fused_computation.21 | custom fusion | flops 4718592 | bytes 4718596
  50.6 7.4 %all-to-all-start.1 = ((bf16[1,32,16,8,384]{4,3,2,0,1:T(8,128)(2,1)}), bf16[1,32,16,8,384]{4,3,2,0,1:T(8,128)(2,1)}, u32[]{:S(2)}, u32[]{:S(2)}) async-start(bf16[1,32,16,8,384]{4,3,2,0,1:T(8,128)(2,1)} %bitcast.42), calls=%async_computation.1 | async-start | bytes 6291456 | tf_op jit(solution)/shard_map/all_to_all | solution.py:45
  58.1 0.1 copy.22
  58.2 37.6 %all-to-all-done.1 = bf16[1,32,16,8,384]{4,3,2,0,1:T(8,128)(2,1)} async-done(((bf16[1,32,16,8,384]{4,3,2,0,1:T(8,128)(2,1)}), bf16[1,32,16,8,384]{4,3,2,0,1:T(8,128)(2,1)}, u32[]{:S(2)}, u32[]{:S(2)}) %all-to-all-start.1) | async-done | bytes 3145760 | tf_op jit(solution)/shard_map/all_to_all | solution.py:45
  95.8 2.4 copy_bitcast_fusion
  98.2 0.7 fusion.19
  98.9 3.1 %fusion.25 = (f32[16,256]{1,0:T(8,128)S(1)}, f32[16,256,256]{1,2,0:T(8,128)S(1)}) fusion(f32[16,256,256]{1,2,0:T(8,128)S(1)} %fusion.19, pred[16,256]{1,0:T(8,128)(4,1)S(1)} %copy.22), kind=kOutput, calls=%fused_computation.50 | output fusion | flops 6291711 | bytes 8409088 | tf_op jit(solution)/shard_map/sub | solution.py:60
  101.9 0.8 fusion.16
  102.7 0.0 copy-start.1
  102.8 1.3 copy.30
  104.0 8.0 %all-to-all-start.2 = ((bf16[1,32,16,8,128]{4,3,2,0,1:T(8,128)(2,1)}), bf16[1,32,16,8,128]{4,3,2,0,1:T(8,128)(2,1)S(1)}, u32[]{:S(2)}, u32[]{:S(2)}) async-start(bf16[1,32,16,8,128]{4,3,2,0,1:T(8,128)(2,1)} %bitcast.40), calls=%async_computation.2 | async-start | bytes 2097152 | tf_op jit(solution)/shard_map/all_to_all | solution.py:70
  112.1 0.0 reduce-scatter.2.cloned.1.call-start
  112.1 2.2 fusion.18
  114.4 0.0 reduce-scatter.2.cloned.1.call-update
  114.4 0.0 all-gather.2.cloned.1.call-start
  114.5 11.6 %all-to-all-done.2 = bf16[1,32,16,8,128]{4,3,2,0,1:T(8,128)(2,1)S(1)} async-done(((bf16[1,32,16,8,128]{4,3,2,0,1:T(8,128)(2,1)}), bf16[1,32,16,8,128]{4,3,2,0,1:T(8,128)(2,1)S(1)}, u32[]{:S(2)}, u32[]{:S(2)}) %all-to-all-start.2) | async-done | bytes 1048608 | tf_op jit(solution)/shard_map/all_to_all | solution.py:70
  126.1 6.2 %gather_fusion = bf16[2048,128]{1,0:T(8,128)(2,1)S(1)} fusion(bf16[4096,128]{1,0:T(8,128)(2,1)S(1)} %bitcast.41, s32[2048]{0:T(1024)S(1)} %broadcast_clamp_fusion), kind=kCustom, calls=%fused_computation | custom fusion | bytes 1056768 | tf_op jit(solution)/shard_map/jit(take_along_axis)/gather | solution.py:72
  132.2 1.1 broadcast_select_fusion
  133.4 0.0 all-gather.2.cloned.1.call-update
  133.4 82.1 %reduce-scatter.2.cloned.1.call-done = bf16[1,16,128]{2,1,0:T(8,128)(2,1)} async-done(((bf16[1,512,128]{2,1,0:T(8,128)(2,1)}), bf16[1,16,128]{2,1,0:T(8,128)(2,1)}) %reduce-scatter.2.cloned.1.call-update) | async-done | bytes 4112 | tf_op jit(solution)/shard_map/reduce_scatter | solution.py:85
  215.5 1.3 multiply_add_fusion
  216.8 49.4 %all-gather.2.cloned.1.call-done = bf16[2048,2048]{1,0:T(8,128)(2,1)} async-done(((bf16[2048,128]{1,0:T(8,128)(2,1)}), bf16[2048,2048]{1,0:T(8,128)(2,1)}) %all-gather.2.cloned.1.call-update) | async-done | bytes 8388624 | tf_op jit(solution)/shard_map/all_gather | solution.py:75
  266.2 6.5 %convolution_convert_fusion = bf16[2048,128]{1,0:T(8,128)(2,1)} fusion(bf16[2048,2048]{1,0:T(8,128)(2,1)} %all-gather.2.cloned.1.call-done, bf16[2048,128]{1,0:T(8,128)(2,1)S(1)} %copy-done), kind=kOutput, calls=%fused_computation.14 | convolution fusion | flops 1074003968 | bytes 9437184 | tf_op jit(solution)/shard_map/dot_general | solution.py:74
  (11 shorter events, 0.1 us)
Async XLA Ops:
  8.0 258.2 %copy-start = (bf16[2048,128]{1,0:T(8,128)(2,1)S(1)}, bf16[2048,128]{1,0:T(8,128)(2,1)}, u32[]{:S(2)}) copy-start(bf16[2048,128]{1,0:T(8,128)(2,1)} %param.10) | copy-start | bytes 1572868
  31.0 19.6 %all-to-all-start = ((bf16[1,32,16,8,1]{2,3,4,0,1:T(8,128)(2,1)}), bf16[1,32,16,8,1]{2,3,4,0,1:T(8,128)(2,1)S(1)}, u32[]{:S(2)}, u32[]{:S(2)}) async-start(bf16[1,32,16,8,1]{2,3,4,0,1:T(8,128)(2,1)} %copy.21), calls=%async_computation | async-start | bytes 131072 | tf_op jit(solution)/shard_map/all_to_all | solution.py:46
  50.6 45.1 %all-to-all-start.1 = ((bf16[1,32,16,8,384]{4,3,2,0,1:T(8,128)(2,1)}), bf16[1,32,16,8,384]{4,3,2,0,1:T(8,128)(2,1)}, u32[]{:S(2)}, u32[]{:S(2)}) async-start(bf16[1,32,16,8,384]{4,3,2,0,1:T(8,128)(2,1)} %bitcast.42), calls=%async_computation.1 | async-start | bytes 6291456 | tf_op jit(solution)/shard_map/all_to_all | solution.py:45
  102.7 9.4 %copy-start.1 = (bf16[2048,128]{1,0:T(8,128)(2,1)S(1)}, bf16[2048,128]{1,0:T(8,128)(2,1)}, u32[]{:S(2)}) copy-start(bf16[2048,128]{1,0:T(8,128)(2,1)} %param.7) | copy-start | bytes 1572868
  102.7 9.4 %copy-start.2 = (s32[1,2048,1]{1,2,0:T(1,128)S(1)}, s32[1,2048,1]{1,2,0:T(1,128)}, u32[]{:S(2)}) copy-start(s32[1,2048,1]{1,2,0:T(1,128)} %param.9) | copy-start | bytes 24580
  104.0 22.0 %all-to-all-start.2 = ((bf16[1,32,16,8,128]{4,3,2,0,1:T(8,128)(2,1)}), bf16[1,32,16,8,128]{4,3,2,0,1:T(8,128)(2,1)S(1)}, u32[]{:S(2)}, u32[]{:S(2)}) async-start(bf16[1,32,16,8,128]{4,3,2,0,1:T(8,128)(2,1)} %bitcast.40), calls=%async_computation.2 | async-start | bytes 2097152 | tf_op jit(solution)/shard_map/all_to_all | solution.py:70
  112.0 103.5 %copy-start.3 = (f32[1,16,128]{2,1,0:T(8,128)S(1)}, f32[1,16,128]{2,1,0:T(8,128)}, u32[]{:S(2)}) copy-start(f32[1,16,128]{2,1,0:T(8,128)} %param.11) | copy-start | bytes 24580
  112.1 103.4 %reduce-scatter.2.cloned.1.call-start = ((), (), s32[]{:S(2)}) async-start(), calls=%async_computation.5 | async-start | bytes 135168 | tf_op jit(solution)/shard_map/reduce_scatter | solution.py:85
  114.4 151.8 %all-gather.2.cloned.1.call-start = ((), (), s32[]{:S(2)}) async-start(), calls=%async_computation.4 | async-start | bytes 8912896 | tf_op jit(solution)/shard_map/all_gather | solution.py:75
Sparse Core Ops, SparseCore 0:
  117.2 98.2 reduce-scatter.1
Sparse Core Ops, SparseCore 1:
  133.5 132.7 all-gather.1
where the time goes:
time: 281 us; the launch traced here: 280 us
  waiting for transfers between devices  181 us (64%)
  local copies, waits for them, and re-layouts  25.4 us (9%)
  other arithmetic  25.1 us (9%)
  starting transfers between devices  23 us (8%)
  between operations  15.6 us (6%)
  matrix products  10.3 us (4%)
    reduce_scatter x1, waiting for transfers between devices, on_device(): lax.psum_scatter(partial_value.astype(jnp.bfloat16), 'ctx', scatter_dimen...  82.1 us
    all_gather x1, waiting for transfers between devices, on_device(): lax.all_gather(attention, 'hg', axis=1, tiled=True)  49.4 us
    all_to_all x1, waiting for transfers between devices, on_device(): lax.all_to_all(outgoing, 'ctx', split_axis=1, concat_axis=1, tiled=True)  37.6 us
    unnamed x10, local copies, waits for them, and re-layouts  14.6 us
    unnamed x4, other arithmetic  13.6 us
    all_to_all x1, waiting for transfers between devices, on_device(): lax.all_to_all(mixed_rows, 'ctx', split_axis=1, concat_axis=1, tiled=True)  11.6 us
    all_to_all x1, starting transfers between devices, on_device(): lax.all_to_all(mixed_rows, 'ctx', split_axis=1, concat_axis=1, tiled=True)  7.99 us
    all_to_all x1, starting transfers between devices, on_device(): lax.all_to_all(live_flags, 'ctx', split_axis=1, concat_axis=1, tiled=True)  7.51 us
  transfers between devices with their start and end apart: 5, of which 4 were waited for; matrix products, arithmetic and copies ran while one was open for 8% of the time, Pallas kernels for 0%

commit v1 on v0

--- a/solution.py
+++ b/solution.py
@@ -14,10 +14,12 @@
 
 def on_device(queries, keys, values, cluster_ids, w_out, old_sums):
     ctx_count = lax.axis_size("ctx")
+    hg_count = lax.axis_size("hg")
     local_count = NCL // ctx_count
     heads_dev = cluster_ids.shape[0]
     tok_rows = queries.shape[0]
     cluster_of = cluster_ids[:, :, 0]
+    w_all = lax.all_gather(w_out, "hg", axis=0, tiled=False)
 
     def split_heads(source):
         return source.reshape(tok_rows, heads_dev, HD).transpose(1, 0, 2)
@@ -65,26 +67,19 @@
     mixed_rows = mixed_rows.reshape(heads_dev, groups, ctx_count, SLOTS, HD).transpose(
         0, 2, 1, 3, 4
     )
-    result = mixed_rows
-    mixed_rows = result
     returned = lax.all_to_all(mixed_rows, "ctx", split_axis=1, concat_axis=1, tiled=True)
     flat_back = returned.reshape(heads_dev, NCL * SLOTS, HD)
     attention = jnp.take_along_axis(flat_back, target[:, :, None], axis=1)
-    attention = attention.transpose(1, 0, 2).reshape(tok_rows, heads_dev * HD)
-    projected = jnp.dot(
-        lax.all_gather(attention, "hg", axis=1, tiled=True),
-        w_out,
-        preferred_element_type=jnp.float32,
+    attention = attention.reshape(heads_dev, hg_count, tok_rows // hg_count, HD)
+    all_heads = lax.all_to_all(attention, "hg", split_axis=1, concat_axis=1, tiled=True)
+    all_heads = all_heads.reshape(hg_count, tok_rows // hg_count, HD)
+    w_all = w_all.reshape(hg_count, hg_count, HD, w_out.shape[1])
+    mixed = jnp.einsum(
+        "htd,nhdf->ntf", all_heads, w_all, preferred_element_type=jnp.float32
     ).astype(jnp.bfloat16)
-    onehot = (cluster_of[:, :, None] == jnp.arange(NCL, dtype=jnp.int32)[None, None, :]).astype(
-        jnp.bfloat16
-    )
-    partial_value = jnp.einsum(
-        "htc,htd->hcd", onehot, packed[..., HD : 2 * HD], preferred_element_type=jnp.float32
-    )
-    member_sums = lax.psum_scatter(
-        partial_value.astype(jnp.bfloat16), "ctx", scatter_dimension=1, tiled=True
-    ).astype(jnp.float32)
+    projected = lax.all_to_all(mixed, "hg", split_axis=0, concat_axis=0, tiled=True)
+    projected = projected.reshape(tok_rows, w_out.shape[1])
+    member_sums = jnp.sum(key_rows.astype(jnp.float32), axis=2)
     centroid_sums = DECAY * old_sums + (1.0 - DECAY) * member_sums
     return (projected, centroid_sums)
 

time: 281 us -> 227 us (0.81)
  the two profiles are of different devices: /device:TPU:74 before, /device:TPU:32 now
where the time goes in v1:
time: 227 us; the launch traced here: 226 us
  waiting for transfers between devices  86.1 us (38%)
  blocking collectives  44 us (19%)
  starting transfers between devices  25.5 us (11%)
  other arithmetic  25 us (11%)
  local copies, waits for them, and re-layouts  24.3 us (11%)
  between operations  14.2 us (6%)
  matrix products  6.94 us (3%)
    all_to_all x1, blocking collectives, on_device(): lax.all_to_all(attention, 'hg', split_axis=1, concat_axis=1, tiled=True)  44 us
    all_to_all x1, waiting for transfers between devices, on_device(): lax.all_to_all(outgoing, 'ctx', split_axis=1, concat_axis=1, tiled=True)  41.5 us
    all_to_all x1, waiting for transfers between devices, on_device(): lax.all_to_all(mixed, 'hg', split_axis=0, concat_axis=0, tiled=True)  26.7 us
    all_to_all x1, waiting for transfers between devices, on_device(): lax.all_to_all(mixed_rows, 'ctx', split_axis=1, concat_axis=1, tiled=True)  17.3 us
    unnamed x7, local copies, waits for them, and re-layouts  15.4 us
    unnamed x4, other arithmetic  13.7 us
    all_to_all x1, starting transfers between devices, on_device(): lax.all_to_all(outgoing, 'ctx', split_axis=1, concat_axis=1, tiled=True)  7.56 us
    all_to_all x1, starting transfers between devices, on_device(): lax.all_to_all(live_flags, 'ctx', split_axis=1, concat_axis=1, tiled=True)  7.32 us
  transfers between devices with their start and end apart: 5, of which 3 were waited for; matrix products, arithmetic and copies ran while one was open for 22% of the time, Pallas kernels for 0%

profile of v1, /device:TPU:32, one launch (start us, length us, event | category | flops | bytes accessed | tf_op | source)
XLA Modules:
  0.0 226.1 jit_solution(16123394473657097860)
XLA Ops:
  7.2 0.0 all-gather.3.cloned.1.call-start
  7.2 0.7 all-gather.3.cloned.1.call-update
  7.9 5.2 %convert_reduce_fusion = s32[2048]{0:T(1024)S(1)} fusion(s32[2048]{0:T(1024)} %bitcast.67), kind=kLoop, calls=%fused_computation.4 | loop fusion | flops 20969472 | bytes 16384 | tf_op jit(solution)/shard_map/while/body/eval_jaxpr/reduce_sum | solution.py:34
  13.1 0.7 and_reduce_fusion.1
  13.9 0.7 fusion.21
  14.6 0.8 and_reduce_fusion
  15.4 14.6 %scatter_custom_fusion = bf16[4096]{0:T(1024)(128)(2,1)S(1)} fusion(s32[2048]{0:T(1024)S(1)} %broadcast_select_fusion.1, bf16[2048]{0:T(1024)(128)(2,1)S(1)} %broadcast.107, bf16[]{:T(256)} %constant.10.clone.1), kind=kCustom, calls=%fused_computation.45 | custom fusion | bytes 8194
  30.0 0.2 reshape.148
  30.2 0.7 copy.22
  30.9 7.3 %all-to-all-start = ((bf16[1,32,16,8,1]{2,3,4,0,1:T(8,128)(2,1)}), bf16[1,32,16,8,1]{2,3,4,0,1:T(8,128)(2,1)S(1)}, u32[]{:S(2)}, u32[]{:S(2)}) async-start(bf16[1,32,16,8,1]{2,3,4,0,1:T(8,128)(2,1)} %copy.22), calls=%async_computation | async-start | bytes 131072 | tf_op jit(solution)/shard_map/all_to_all | solution.py:48
  38.2 12.2 %scatter_custom_fusion.1 = bf16[4096,384]{1,0:T(8,128)(2,1)} fusion(s32[2048]{0:T(1024)S(1)} %broadcast_select_fusion.1, bf16[1,2048,128]{2,1,0:T(8,128)(2,1)} %bitcast.62, bf16[]{:T(256)} %constant.67, bf16[1,2048,128]{2,1,0:T(8,128)(2,1)} %bitcast.63, bf16[1,2048,128]{2,1,0:T(8,128)(2,1)} %bitcast.64, bf16[]{:T(256)} %constant.10.clone.1), kind=kCustom, calls=%fused_computation.18 | custom fusion | flops 4718592 | bytes 4718596
  50.4 0.0 all-to-all-done
  50.4 7.6 %all-to-all-start.1 = ((bf16[1,32,16,8,384]{4,3,2,0,1:T(8,128)(2,1)}), bf16[1,32,16,8,384]{4,3,2,0,1:T(8,128)(2,1)S(1)}, u32[]{:S(2)}, u32[]{:S(2)}) async-start(bf16[1,32,16,8,384]{4,3,2,0,1:T(8,128)(2,1)} %bitcast.9), calls=%async_computation.1 | async-start | bytes 6291456 | tf_op jit(solution)/shard_map/all_to_all | solution.py:47
  58.0 0.1 copy.23
  58.1 41.5 %all-to-all-done.1 = bf16[1,32,16,8,384]{4,3,2,0,1:T(8,128)(2,1)S(1)} async-done(((bf16[1,32,16,8,384]{4,3,2,0,1:T(8,128)(2,1)}), bf16[1,32,16,8,384]{4,3,2,0,1:T(8,128)(2,1)S(1)}, u32[]{:S(2)}, u32[]{:S(2)}) %all-to-all-start.1) | async-done | bytes 3145760 | tf_op jit(solution)/shard_map/all_to_all | solution.py:47
  99.6 0.5 copy_bitcast_fusion
  100.0 0.0 copy-start
  100.1 0.7 fusion.17
  100.8 3.1 %fusion.26 = (f32[16,256]{1,0:T(8,128)S(1)}, f32[16,256,256]{1,2,0:T(8,128)S(1)}) fusion(f32[16,256,256]{1,2,0:T(8,128)S(1)} %fusion.17, pred[16,256]{1,0:T(8,128)(4,1)S(1)} %copy.23), kind=kOutput, calls=%fused_computation.50 | output fusion | flops 6291711 | bytes 8409088 | tf_op jit(solution)/shard_map/sub | solution.py:62
  103.8 0.8 fusion.14
  104.6 1.3 copy.33
  105.9 3.9 %all-to-all-start.2 = ((bf16[1,32,16,8,128]{4,3,2,0,1:T(8,128)(2,1)}), bf16[1,32,16,8,128]{4,3,2,0,1:T(8,128)(2,1)S(1)}, u32[]{:S(2)}, u32[]{:S(2)}) async-start(bf16[1,32,16,8,128]{4,3,2,0,1:T(8,128)(2,1)} %bitcast.57), calls=%async_computation.2 | async-start | bytes 2097152 | tf_op jit(solution)/shard_map/all_to_all | solution.py:70
  109.8 17.3 %all-to-all-done.2 = bf16[1,32,16,8,128]{4,3,2,0,1:T(8,128)(2,1)S(1)} async-done(((bf16[1,32,16,8,128]{4,3,2,0,1:T(8,128)(2,1)}), bf16[1,32,16,8,128]{4,3,2,0,1:T(8,128)(2,1)S(1)}, u32[]{:S(2)}, u32[]{:S(2)}) %all-to-all-start.2) | async-done | bytes 1048608 | tf_op jit(solution)/shard_map/all_to_all | solution.py:70
  127.2 6.2 %gather_fusion = bf16[2048,128]{1,0:T(8,128)(2,1)S(1)} fusion(bf16[4096,128]{1,0:T(8,128)(2,1)S(1)} %bitcast.58, s32[2048]{0:T(1024)S(1)} %broadcast_clamp_fusion), kind=kCustom, calls=%fused_computation | custom fusion | bytes 1056768 | tf_op jit(solution)/shard_map/jit(take_along_axis)/gather | solution.py:72
  133.4 0.3 broadcast_select_fusion
  133.7 44.0 %all_to_all.25 = bf16[1,16,128,128]{3,2,0,1:T(8,128)(2,1)S(1)} all-to-all(bf16[1,16,128,128]{3,2,0,1:T(8,128)(2,1)S(1)} %broadcast_select_fusion), channel_id=1, replica_groups=mesh['ctx'=32,'hg'=16] {'hg'}, dimensions={1} | all-to-all | bytes 1048576 | tf_op jit(solution)/shard_map/all_to_all | solution.py:74
  177.7 5.4 %fusion.16 = bf16[16,128,128]{2,1,0:T(8,128)(2,1)} fusion(bf16[16,16,128,128]{3,2,1,0:T(8,128)(2,1)} %bitcast.59, bf16[1,16,128,128]{3,2,0,1:T(8,128)(2,1)S(1)} %all_to_all.25), kind=kOutput, calls=%fused_computation.28 | convolution fusion | flops 1074003968 | bytes 9437184 | tf_op jit(solution)/shard_map/htd,nhdf->ntf/dot_general | solution.py:77
  183.2 6.6 %all-to-all-start.4 = ((bf16[16,128,128]{2,1,0:T(8,128)(2,1)}), bf16[16,128,128]{2,1,0:T(8,128)(2,1)S(1)}, u32[]{:S(2)}, u32[]{:S(2)}) async-start(bf16[16,128,128]{2,1,0:T(8,128)(2,1)} %fusion.16), calls=%async_computation.4 | async-start | bytes 1048576 | tf_op jit(solution)/shard_map/all_to_all | solution.py:80
  189.8 1.4 convert_reduce_fusion.1
  191.2 0.6 bitcast_add_fusion
  191.8 26.7 %all-to-all-done.4 = bf16[16,128,128]{2,1,0:T(8,128)(2,1)S(1)} async-done(((bf16[16,128,128]{2,1,0:T(8,128)(2,1)}), bf16[16,128,128]{2,1,0:T(8,128)(2,1)S(1)}, u32[]{:S(2)}, u32[]{:S(2)}) %all-to-all-start.4) | async-done | bytes 524320 | tf_op jit(solution)/shard_map/all_to_all | solution.py:80
  218.5 0.8 copy.35
  (8 shorter events, 0.0 us)
Async XLA Ops:
  7.2 170.6 %all-gather.3.cloned.1.call-start = ((), (), s32[]{:S(2)}) async-start(), calls=%async_computation.5 | async-start | bytes 8912896 | tf_op jit(solution)/shard_map/all_gather | solution.py:22
  30.9 19.5 %all-to-all-start = ((bf16[1,32,16,8,1]{2,3,4,0,1:T(8,128)(2,1)}), bf16[1,32,16,8,1]{2,3,4,0,1:T(8,128)(2,1)S(1)}, u32[]{:S(2)}, u32[]{:S(2)}) async-start(bf16[1,32,16,8,1]{2,3,4,0,1:T(8,128)(2,1)} %copy.22), calls=%async_computation | async-start | bytes 131072 | tf_op jit(solution)/shard_map/all_to_all | solution.py:48
  50.4 49.2 %all-to-all-start.1 = ((bf16[1,32,16,8,384]{4,3,2,0,1:T(8,128)(2,1)}), bf16[1,32,16,8,384]{4,3,2,0,1:T(8,128)(2,1)S(1)}, u32[]{:S(2)}, u32[]{:S(2)}) async-start(bf16[1,32,16,8,384]{4,3,2,0,1:T(8,128)(2,1)} %bitcast.9), calls=%async_computation.1 | async-start | bytes 6291456 | tf_op jit(solution)/shard_map/all_to_all | solution.py:47
  100.0 3.8 %copy-start = (bf16[1,16,256,384]{3,2,1,0:T(8,128)(2,1)}, bf16[1,16,256,384]{3,2,1,0:T(8,128)(2,1)S(1)}, u32[]{:S(2)}) copy-start(bf16[1,16,256,384]{3,2,1,0:T(8,128)(2,1)S(1)} %copy_bitcast_fusion) | copy-start | bytes 9437188
  105.9 21.3 %all-to-all-start.2 = ((bf16[1,32,16,8,128]{4,3,2,0,1:T(8,128)(2,1)}), bf16[1,32,16,8,128]{4,3,2,0,1:T(8,128)(2,1)S(1)}, u32[]{:S(2)}, u32[]{:S(2)}) async-start(bf16[1,32,16,8,128]{4,3,2,0,1:T(8,128)(2,1)} %bitcast.57), calls=%async_computation.2 | async-start | bytes 2097152 | tf_op jit(solution)/shard_map/all_to_all | solution.py:70
  177.7 13.5 %copy-start.1 = (f32[1,16,128]{2,1,0:T(8,128)S(1)}, f32[1,16,128]{2,1,0:T(8,128)}, u32[]{:S(2)}) copy-start(f32[1,16,128]{2,1,0:T(8,128)} %param.11) | copy-start | bytes 24580
  183.2 35.3 %all-to-all-start.4 = ((bf16[16,128,128]{2,1,0:T(8,128)(2,1)}), bf16[16,128,128]{2,1,0:T(8,128)(2,1)S(1)}, u32[]{:S(2)}, u32[]{:S(2)}) async-start(bf16[16,128,128]{2,1,0:T(8,128)(2,1)} %fusion.16), calls=%async_computation.4 | async-start | bytes 1048576 | tf_op jit(solution)/shard_map/all_to_all | solution.py:80
Sparse Core Ops, SparseCore 0:
  10.1 107.7 all-gather.2

commit v2 on v1

v2 whole, which is shorter than its diff:
```python
import jax
import jax.numpy as jnp
from jax import lax
from jax.experimental import pallas as pl
from jax.experimental.pallas import tpu as pltpu
from jax.sharding import PartitionSpec as P

HD = 128
NCL = 512
SLOTS = 8
CTX = 32
LOCAL = NCL // CTX
PAIR = LOCAL * SLOTS
TILE = 128

DECAY = 0.9
NEG_FILL = -1e30
EMPTY = 1024.0

F32 = jnp.float32
BF16 = jnp.bfloat16


def place_kernel(ids_ref, q_ref, k_ref, v_ref, out_ref, target_ref, rows, slot_hot, dest_row):
    step = pl.program_id(0)
    per_step = out_ref.shape[0]
    tokens = ids_ref.shape[1]

    @pl.when(step == 0)
    def _():
        ids = ids_ref[...]
        wide = ids.astype(F32)
        before = lax.broadcasted_iota(jnp.int32, (TILE, TILE), 0) < lax.broadcasted_iota(
            jnp.int32, (TILE, TILE), 1
        )
        columns = [wide[:, i * TILE : (i + 1) * TILE] for i in range(tokens // TILE)]
        down = [jnp.transpose(jnp.broadcast_to(c, (TILE, TILE))) for c in columns]
        ranks = []
        for j, column in enumerate(columns):
            here = jnp.broadcast_to(column, (TILE, TILE))
            same = jnp.where((down[j] == here) & before, 1.0, 0.0)
            for i in range(j):
                same = same + jnp.where(down[i] == here, 1.0, 0.0)
            ranks.append(jnp.sum(same, axis=0, keepdims=True))
        rank = jnp.concatenate(ranks, axis=1).astype(jnp.int32)
        target_ref[...] = ids * SLOTS + rank
        slot = (ids % LOCAL) * SLOTS + rank
        slots = lax.broadcasted_iota(jnp.int32, (PAIR, tokens), 0)
        slot_hot[...] = jnp.where(slots == slot, 1.0, 0.0).astype(BF16)
        dest_row[...] = ids // LOCAL
        rows[:, 0:HD] = q_ref[...]
        rows[:, HD : 2 * HD] = k_ref[...]
        rows[:, 2 * HD : 3 * HD] = v_ref[...]
        rows[:, 3 * HD : 4 * HD] = jnp.ones((tokens, HD), BF16)

    first_lane = lax.broadcasted_iota(jnp.int32, (PAIR, HD), 1) == 0
    for i in range(per_step):
        mine = jnp.where(dest_row[...] == step * per_step + i, 1.0, 0.0)
        mine = jnp.broadcast_to(mine, (16, tokens)).astype(BF16)
        hot = slot_hot[...].reshape(PAIR // 16, 16, tokens) * mine[None]
        placed = jnp.dot(hot.reshape(PAIR, tokens), rows[...], preferred_element_type=F32)
        filled = placed[:, 3 * HD : 4 * HD]
        mark = jnp.where(first_lane, EMPTY * (1.0 - filled), 0.0)
        out_ref[i, 0] = placed[:, 0:HD].astype(BF16)
        out_ref[i, 1] = (placed[:, HD : 2 * HD] + mark).astype(BF16)
        out_ref[i, 2] = placed[:, 2 * HD : 3 * HD].astype(BF16)


def place(ids_row, queries, keys, values, per_step=2):
    tokens = queries.shape[0]
    whole = pl.BlockSpec((tokens, HD), lambda s: (0, 0))
    line = pl.BlockSpec((1, tokens), lambda s: (0, 0))
    return pl.pallas_call(
        place_kernel,
        grid=(CTX // per_step,),
        out_shape=(
            jax.ShapeDtypeStruct((CTX, 3, PAIR, HD), BF16),
            jax.ShapeDtypeStruct((1, tokens), jnp.int32),
        ),
        in_specs=[line, whole, whole, whole],
        out_specs=(pl.BlockSpec((per_step, 3, PAIR, HD), lambda s: (s, 0, 0, 0)), line),
        scratch_shapes=[
            pltpu.VMEM((tokens, 4 * HD), BF16),
            pltpu.VMEM((PAIR, tokens), BF16),
            pltpu.VMEM((1, tokens), jnp.int32),
        ],
        compiler_params=pltpu.CompilerParams(
            dimension_semantics=("arbitrary",), vmem_limit_bytes=32 << 20
        ),
        cost_estimate=pl.CostEstimate(
            flops=2 * NCL * SLOTS * tokens * 4 * HD, bytes_accessed=5 << 20, transcendentals=0
        ),
        name="place",
    )(ids_row, queries, keys, values)


def attend_kernel(q_ref, k_ref, v_ref, old_ref, out_ref, sums_ref):
    step = pl.program_id(0)
    sources = q_ref.shape[0]
    members = sources * SLOTS

    def halves(ref):
        both = ref[...].reshape(sources, 2 * SLOTS, HD).astype(F32)
        return [
            both[:, i * SLOTS : (i + 1) * SLOTS].reshape(members, HD).astype(BF16)
            for i in range(2)
        ]

    first_lane = (lax.broadcasted_iota(jnp.int32, (16, HD), 1) == 0).astype(BF16)
    dims = (((1,), (1,)), ((), ()))
    mixed, sums = [], []
    for q, k, v in zip(halves(q_ref), halves(k_ref), halves(v_ref)):
        marks = lax.dot_general(first_lane, k, dims, preferred_element_type=F32)
        present = marks < 0.5 * EMPTY
        scores = lax.dot_general(q, k, dims, preferred_element_type=F32) * HD ** (-0.5)
        scores = jnp.where(present[0:1], scores, NEG_FILL)
        weights = jnp.exp(scores - jnp.max(scores, axis=1, keepdims=True))
        share = weights / jnp.sum(weights, axis=1, keepdims=True)
        mixed.append(
            jnp.dot(share.astype(BF16), v, preferred_element_type=F32).reshape(sources, SLOTS, HD)
        )
        live = jnp.where(present, 1.0, 0.0).astype(BF16)
        sums.append(jnp.dot(live, k, preferred_element_type=F32)[0:1])
    out_ref[...] = jnp.concatenate(mixed, axis=1).astype(BF16)
    member_sums = jnp.concatenate(sums, axis=0)
    two = pl.ds(2 * step, 2)
    sums_ref[two, :] = DECAY * old_ref[two, :] + (1.0 - DECAY) * member_sums


def attend(slab, old_sums):
    def part(which):
        return pl.BlockSpec((CTX, 1, 2 * SLOTS, HD), lambda s: (0, which, s, 0))

    cell = pl.BlockSpec((LOCAL, HD), lambda s: (0, 0))
    return pl.pallas_call(
        attend_kernel,
        grid=(LOCAL // 2,),
        out_shape=(
            jax.ShapeDtypeStruct((CTX, PAIR, HD), BF16),
            jax.ShapeDtypeStruct((LOCAL, HD), F32),
        ),
        in_specs=[part(0), part(1), part(2), cell],
        out_specs=(pl.BlockSpec((CTX, 2 * SLOTS, HD), lambda s: (0, s, 0)), cell),
        compiler_params=pltpu.CompilerParams(
            dimension_semantics=("arbitrary",), vmem_limit_bytes=32 << 20
        ),
        cost_estimate=pl.CostEstimate(
            flops=4 * LOCAL * 256 * 256 * HD,
            bytes_accessed=5 << 20,
            transcendentals=LOCAL * 256 * 256,
        ),
        name="attend",
    )(slab, slab, slab, old_sums)


def on_device(queries, keys, values, cluster_ids, w_out, old_sums):
    hg_count = lax.axis_size("hg")
    tok_rows = queries.shape[0]
    w_all = lax.all_gather(w_out, "hg", axis=0, tiled=False)
    outgoing, target = place(cluster_ids[:, :, 0], queries, keys, values)
    slab = lax.all_to_all(outgoing, "ctx", split_axis=0, concat_axis=0, tiled=True)
    mixed_rows, centroid_sums = attend(slab, old_sums[0])
    returned = lax.all_to_all(mixed_rows, "ctx", split_axis=0, concat_axis=0, tiled=True)
    flat_back = returned.reshape(NCL * SLOTS, HD)
    attention = jnp.take(flat_back, target[0], axis=0, mode="clip")
    attention = attention.reshape(hg_count, tok_rows // hg_count, HD)
    all_heads = lax.all_to_all(attention, "hg", split_axis=0, concat_axis=0, tiled=True)
    w_all = w_all.reshape(hg_count, hg_count, HD, w_out.shape[1])
    mixed = jnp.einsum("htd,nhdf->ntf", all_heads, w_all, preferred_element_type=F32).astype(BF16)
    projected = lax.all_to_all(mixed, "hg", split_axis=0, concat_axis=0, tiled=True)
    return (projected.reshape(tok_rows, w_out.shape[1]), centroid_sums[None])


def solution(mesh):
    placed = (
        P("ctx", "hg"),
        P("ctx", "hg"),
        P("ctx", "hg"),
        P("hg", "ctx", None),
        P(None, "hg"),
        P("hg", "ctx", None),
    )
    return jax.shard_map(
        on_device,
        mesh=mesh,
        in_specs=placed,
        out_specs=(P("ctx", "hg"), P("hg", "ctx", None)),
        check_vma=False,
    )
```

time: 227 us -> 200 us (0.88)
  the two profiles are of different devices: /device:TPU:32 before, /device:TPU:2 now
where the time goes in v2:
time: 200 us; the launch traced here: 199 us
  blocking collectives  126 us (63%)
  Pallas kernels  22 us (11%)
  waiting for transfers between devices  16.9 us (8%)
  between operations  14.1 us (7%)
  local copies, waits for them, and re-layouts  10.8 us (5%)
  starting transfers between devices  5.08 us (3%)
  matrix products  4.64 us (2%)
    all_to_all x1, blocking collectives, on_device(): lax.all_to_all(outgoing, 'ctx', split_axis=0, concat_axis=0, tiled=True)  47.3 us
    all_to_all x1, blocking collectives, on_device(): lax.all_to_all(attention, 'hg', split_axis=0, concat_axis=0, tiled=True)  43 us
    all_to_all x1, blocking collectives, on_device(): lax.all_to_all(mixed, 'hg', split_axis=0, concat_axis=0, tiled=True)  35.5 us
    all_to_all x1, waiting for transfers between devices, on_device(): lax.all_to_all(mixed_rows, 'ctx', split_axis=0, concat_axis=0, tiled=True)  16.2 us
    pallas_call x1, Pallas kernels, place(): pl.pallas_call(place_kernel, grid=(CTX // per_step,), out_shape=(jax.Shap...  13.2 us
    pallas_call x1, Pallas kernels, attend(): pl.pallas_call(attend_kernel, grid=(LOCAL // 2,), out_shape=(jax.ShapeDty...  8.84 us
    gather x1, local copies, waits for them, and re-layouts, on_device(): attention = jnp.take(flat_back, target[0], axis=0, mode='clip')  6.18 us
    all_to_all x1, starting transfers between devices, on_device(): lax.all_to_all(mixed_rows, 'ctx', split_axis=0, concat_axis=0, tiled=True)  5.04 us
  transfers between devices with their start and end apart: 2, of which 1 were waited for; matrix products, arithmetic and copies ran while one was open for 3% of the time, Pallas kernels for 11%

profile of v2, /device:TPU:2, one launch (start us, length us, event | category | flops | bytes accessed | tf_op | source)
XLA Modules:
  0.0 199.2 jit_solution(2051544198419802994)
XLA Ops:
  7.2 0.0 all-gather.3.cloned.1.call-start
  7.2 0.7 all-gather.3.cloned.1.call-update
  7.9 0.0 copy-start.1
  7.9 1.0 copy-done.1
  8.9 0.0 copy-start.2
  8.9 1.0 copy-done.2
  10.0 0.0 copy-start.3
  10.0 1.0 copy-done.3
  11.0 0.0 copy-start.4
  11.0 0.7 copy-done.4
  11.7 0.0 copy-start
  11.7 13.2 %place.1 = (bf16[32,3,128,128]{3,2,1,0:T(8,128)(2,1)S(1)}, s32[1,2048]{1,0:T(1,128)S(1)}) custom-call(s32[1,2048]{1,0:T(1,128)S(1)} %bitcast.23, bf16[2048,128]{1,0:T(8,128)(2,1)S(1)} %copy-done.1, bf16[2048,128]{1,0:T(8,128)(2,1)S(1)} %copy-done.2, bf16[2048,128]{1,0:T(8,128)(2,1)S(1)} %copy-done.3), custom_call_target="tpu_custom_call" | custom-call | flops 8589934592 | bytes 5242880 | tf_op jit(solution)/shard_map/place/pallas_call | solution.py:73
  24.9 47.3 %all_to_all.20.q_ref.k_ref.v_ref = bf16[32,3,128,128]{3,2,1,0:T(8,128)(2,1)S(1)} all-to-all(bf16[32,3,128,128]{3,2,1,0:T(8,128)(2,1)S(1)} %get-tuple-element.6), channel_id=1, replica_groups=mesh['ctx'=32,'hg'=16] {'ctx'}, dimensions={0} | all-to-all | bytes 6291456 | tf_op jit(solution)/shard_map/all_to_all | solution.py:161
  72.2 0.0 copy-done
  72.2 8.8 %attend.1 = (bf16[32,128,128]{2,1,0:T(8,128)(2,1)}, f32[16,128]{1,0:T(8,128)}) custom-call(bf16[32,3,128,128]{3,2,1,0:T(8,128)(2,1)S(1)} %all_to_all.20.q_ref.k_ref.v_ref, bf16[32,3,128,128]{3,2,1,0:T(8,128)(2,1)S(1)} %all_to_all.20.q_ref.k_ref.v_ref, bf16[32,3,128,128]{3,2,1,0:T(8,128)(2,1)S(1)} %all_to_all.20.q_ref.k_ref.v_ref, f32[16,128]{1,0:T(8,128)S(1)} %bitcast.22), custom_call_target="tpu_custom_call" | custom-call | flops 536870912 | bytes 5242880 | tf_op jit(solution)/shard_map/attend/pallas_call | solution.py:135
  81.0 5.0 %all-to-all-start.1 = ((bf16[32,128,128]{2,1,0:T(8,128)(2,1)}), bf16[32,128,128]{2,1,0:T(8,128)(2,1)S(1)}, u32[]{:S(2)}, u32[]{:S(2)}) async-start(bf16[32,128,128]{2,1,0:T(8,128)(2,1)} %get-tuple-element.7), calls=%async_computation.1 | async-start | bytes 2097152 | tf_op jit(solution)/shard_map/all_to_all | solution.py:163
  86.1 16.2 %all-to-all-done.1 = bf16[32,128,128]{2,1,0:T(8,128)(2,1)S(1)} async-done(((bf16[32,128,128]{2,1,0:T(8,128)(2,1)}), bf16[32,128,128]{2,1,0:T(8,128)(2,1)S(1)}, u32[]{:S(2)}, u32[]{:S(2)}) %all-to-all-start.1) | async-done | bytes 1048608 | tf_op jit(solution)/shard_map/all_to_all | solution.py:163
  102.3 6.2 %gather_fusion = bf16[2048,128]{1,0:T(8,128)(2,1)S(1)} fusion(bf16[4096,128]{1,0:T(8,128)(2,1)S(1)} %bitcast.24, s32[2048]{0:T(1024)S(1)} %broadcast_clamp_fusion), kind=kCustom, calls=%fused_computation | custom fusion | bytes 1056768 | tf_op jit(solution)/shard_map/jit(_take)/gather | solution.py:165
  108.5 43.0 %all_to_all.21 = bf16[16,128,128]{2,1,0:T(8,128)(2,1)S(1)} all-to-all(bf16[16,128,128]{2,1,0:T(8,128)(2,1)S(1)} %bitcast.26), channel_id=1, replica_groups=mesh['ctx'=32,'hg'=16] {'hg'}, dimensions={0} | all-to-all | bytes 1048576 | tf_op jit(solution)/shard_map/all_to_all | solution.py:167
  151.5 0.0 all-gather.3.cloned.1.call-done
  151.5 4.6 %fusion.1 = bf16[16,128,128]{2,1,0:T(8,128)(2,1)S(1)} fusion(bf16[16,16,128,128]{3,2,1,0:T(8,128)(2,1)} %bitcast.25, bf16[16,128,128]{2,1,0:T(8,128)(2,1)S(1)} %all_to_all.21), kind=kOutput, calls=%fused_computation.3 | convolution fusion | flops 1074003968 | bytes 9437184 | tf_op jit(solution)/shard_map/htd,nhdf->ntf/dot_general | solution.py:169
  156.1 35.5 %all_to_all.22 = bf16[16,128,128]{2,1,0:T(8,128)(2,1)S(1)} all-to-all(bf16[16,128,128]{2,1,0:T(8,128)(2,1)S(1)} %fusion.1), channel_id=1, replica_groups=mesh['ctx'=32,'hg'=16] {'hg'}, dimensions={0} | all-to-all | bytes 1048576 | tf_op jit(solution)/shard_map/all_to_all | solution.py:170
  191.6 0.8 copy.10
  (1 shorter events, 0.0 us)
Async XLA Ops:
  7.2 144.3 %all-gather.3.cloned.1.call-start = ((), (), s32[]{:S(2)}) async-start(), calls=%async_computation.4 | async-start | bytes 8912896 | tf_op jit(solution)/shard_map/all_gather | solution.py:159
  7.9 1.0 copy-start.1
  8.9 1.0 copy-start.2
  10.0 1.0 copy-start.3
  11.0 0.7 copy-start.4
  11.7 60.5 %copy-start = (f32[1,16,128]{2,1,0:T(8,128)S(1)}, f32[1,16,128]{2,1,0:T(8,128)}, u32[]{:S(2)}) copy-start(f32[1,16,128]{2,1,0:T(8,128)} %param.11) | copy-start | bytes 24580
  81.0 21.3 %all-to-all-start.1 = ((bf16[32,128,128]{2,1,0:T(8,128)(2,1)}), bf16[32,128,128]{2,1,0:T(8,128)(2,1)S(1)}, u32[]{:S(2)}, u32[]{:S(2)}) async-start(bf16[32,128,128]{2,1,0:T(8,128)(2,1)} %get-tuple-element.7), calls=%async_computation.1 | async-start | bytes 2097152 | tf_op jit(solution)/shard_map/all_to_all | solution.py:163
Sparse Core Ops, SparseCore 0:
  10.1 110.4 all-gather.2

commit v3 on v2

v3 whole, which is shorter than its diff:
```python
import jax
import jax.numpy as jnp
from jax import lax
from jax.experimental import pallas as pl
from jax.experimental.pallas import tpu as pltpu
from jax.sharding import PartitionSpec as P

HD = 128
NCL = 512
SLOTS = 8
CTX = 32
LOCAL = NCL // CTX
PAIR = LOCAL * SLOTS
TILE = 128

DECAY = 0.9
NEG_FILL = -1e30
EMPTY = 1024.0

EXP2_SCALE = HD ** (-0.5) * 1.4426950408889634

F32 = jnp.float32
BF16 = jnp.bfloat16


def place_kernel(
    core_ref, ids_ref, q_ref, k_ref, v_ref, w_ref, out_ref, target_ref, half_ref, rows, slot_hot, hot, dest_row
):
    del core_ref
    step = pl.program_id(0)
    per_step = out_ref.shape[0]
    tokens = ids_ref.shape[1]

    @pl.when(step == 0)
    def _():
        ids = ids_ref[...]
        wide = ids.astype(F32)
        before = lax.broadcasted_iota(jnp.int32, (TILE, TILE), 0) < lax.broadcasted_iota(
            jnp.int32, (TILE, TILE), 1
        )
        columns = [wide[:, i * TILE : (i + 1) * TILE] for i in range(tokens // TILE)]
        down = [jnp.transpose(jnp.broadcast_to(c, (TILE, TILE))) for c in columns]
        ranks = []
        for j, column in enumerate(columns):
            here = jnp.broadcast_to(column, (TILE, TILE))
            same = jnp.where((down[j] == here) & before, 1.0, 0.0)
            for i in range(j):
                same = same + jnp.where(down[i] == here, 1.0, 0.0)
            ranks.append(jnp.sum(same, axis=0, keepdims=True))
        rank = jnp.concatenate(ranks, axis=1).astype(jnp.int32)
        target_ref[...] = ids * SLOTS + rank
        half_ref[...] = w_ref[...]
        slot = (ids % LOCAL) * SLOTS + rank
        slots = lax.broadcasted_iota(jnp.int32, (PAIR, tokens), 0)
        slot_hot[...] = jnp.where(slots == slot, 1.0, 0.0).astype(BF16)
        dest_row[...] = ids // LOCAL
        rows[:, 0:HD] = k_ref[...]
        rows[:, HD : 2 * HD] = jnp.ones((tokens, HD), BF16)
        rows[:, 2 * HD : 3 * HD] = q_ref[...]
        rows[:, 3 * HD : 4 * HD] = v_ref[...]

    for i in range(per_step):
        mine = jnp.where(dest_row[...] == step * per_step + i, 1.0, 0.0)
        mine = jnp.broadcast_to(mine, (16, tokens)).astype(BF16)
        here = slot_hot[...].reshape(PAIR // 16, 16, tokens) * mine[None]
        hot[i * PAIR : (i + 1) * PAIR, :] = here.reshape(PAIR, tokens)
    shape = (per_step, PAIR, HD)
    keyed = jnp.dot(hot[...], rows[:, 0 : 2 * HD], preferred_element_type=F32)
    filled = keyed[:, HD : 2 * HD]
    first_lane = lax.broadcasted_iota(jnp.int32, filled.shape, 1) == 0
    marked = keyed[:, 0:HD] + jnp.where(first_lane, EMPTY * (1.0 - filled), 0.0)
    out_ref[:, 1] = marked.astype(BF16).reshape(shape)
    others = jnp.dot(hot[...], rows[:, 2 * HD : 4 * HD], preferred_element_type=F32)
    out_ref[:, 0] = others[:, 0:HD].astype(BF16).reshape(shape)
    out_ref[:, 2] = others[:, HD : 2 * HD].astype(BF16).reshape(shape)


def place(core, ids_row, queries, keys, values, w_out, per_step=8):
    tokens = queries.shape[0]
    half = w_out.shape[0] // 2
    whole = pl.BlockSpec((tokens, HD), lambda s, c: (0, 0))
    line = pl.BlockSpec((1, tokens), lambda s, c: (0, 0))
    return pl.pallas_call(
        place_kernel,
        grid_spec=pltpu.PrefetchScalarGridSpec(
            num_scalar_prefetch=1,
            grid=(CTX // per_step,),
            in_specs=[
                line,
                whole,
                whole,
                whole,
                pl.BlockSpec((half, w_out.shape[1]), lambda s, c: (c[0], 0)),
            ],
            out_specs=(
                pl.BlockSpec((per_step, 3, PAIR, HD), lambda s, c: (s, 0, 0, 0)),
                line,
                pl.BlockSpec((half, w_out.shape[1]), lambda s, c: (0, 0)),
            ),
            scratch_shapes=[
                pltpu.VMEM((tokens, 4 * HD), BF16),
                pltpu.VMEM((PAIR, tokens), BF16),
                pltpu.VMEM((per_step * PAIR, tokens), BF16),
                pltpu.VMEM((1, tokens), jnp.int32),
            ],
        ),
        out_shape=(
            jax.ShapeDtypeStruct((CTX, 3, PAIR, HD), BF16),
            jax.ShapeDtypeStruct((1, tokens), jnp.int32),
            jax.ShapeDtypeStruct((half, w_out.shape[1]), BF16),
        ),
        compiler_params=pltpu.CompilerParams(
            dimension_semantics=("arbitrary",), vmem_limit_bytes=60 << 20
        ),
        cost_estimate=pl.CostEstimate(
            flops=2 * NCL * SLOTS * tokens * 4 * HD, bytes_accessed=5 << 20, transcendentals=0
        ),
        name="place",
    )(core, ids_row, queries, keys, values, w_out)


def attend_kernel(q_ref, k_ref, v_ref, old_ref, out_ref, sums_ref):
    step = pl.program_id(0)
    sources, block = q_ref.shape[0], q_ref.shape[2]
    count = block // SLOTS
    members = sources * SLOTS

    def split(ref):
        whole = ref[...].reshape(sources, block, HD).astype(F32)
        return [
            whole[:, i * SLOTS : (i + 1) * SLOTS].reshape(members, HD).astype(BF16)
            for i in range(count)
        ]

    first_lane = (lax.broadcasted_iota(jnp.int32, (16, HD), 1) == 0).astype(BF16)
    ones = jnp.ones((members, HD), BF16)
    dims = (((1,), (1,)), ((), ()))
    mixed, sums = [], []
    for q, k, v in zip(split(q_ref), split(k_ref), split(v_ref)):
        marks = lax.dot_general(first_lane, k, dims, preferred_element_type=F32)
        present = marks < 0.5 * EMPTY
        scores = lax.dot_general(q, k, dims, preferred_element_type=F32)
        scores = jnp.where(present[0:1], scores, NEG_FILL)
        weights = jnp.exp2((scores - jnp.max(scores, axis=1, keepdims=True)) * EXP2_SCALE)
        totals = jnp.dot(
            weights.astype(BF16), jnp.concatenate([v, ones], axis=1), preferred_element_type=F32
        )
        mixed.append((totals[:, 0:HD] / totals[:, HD:]).reshape(sources, SLOTS, HD))
        live = jnp.where(present, 1.0, 0.0).astype(BF16)
        sums.append(jnp.dot(live, k, preferred_element_type=F32)[0:1])
    out_ref[...] = jnp.concatenate(mixed, axis=1).astype(BF16)
    member_sums = jnp.concatenate(sums, axis=0)
    these = pl.ds(count * step, count)
    sums_ref[these, :] = DECAY * old_ref[these, :] + (1.0 - DECAY) * member_sums


def attend(slab, old_sums, count=4):
    def part(which):
        return pl.BlockSpec((CTX, 1, count * SLOTS, HD), lambda s: (0, which, s, 0))

    cell = pl.BlockSpec((LOCAL, HD), lambda s: (0, 0))
    return pl.pallas_call(
        attend_kernel,
        grid=(LOCAL // count,),
        out_shape=(
            jax.ShapeDtypeStruct((CTX, PAIR, HD), BF16),
            jax.ShapeDtypeStruct((LOCAL, HD), F32),
        ),
        in_specs=[part(0), part(1), part(2), cell],
        out_specs=(pl.BlockSpec((CTX, count * SLOTS, HD), lambda s: (0, s, 0)), cell),
        compiler_params=pltpu.CompilerParams(
            dimension_semantics=("arbitrary",), vmem_limit_bytes=32 << 20
        ),
        cost_estimate=pl.CostEstimate(
            flops=4 * LOCAL * 256 * 256 * HD,
            bytes_accessed=5 << 20,
            transcendentals=LOCAL * 256 * 256,
        ),
        name="attend",
    )(slab, slab, slab, old_sums)


def fetch_kernel(target_ref, back_ref, out_ref):
    tokens = out_ref.shape[0]
    lanes = lax.broadcasted_iota(jnp.int32, (TILE, PAIR), 1)
    for j in range(tokens // TILE):
        here = target_ref[:, j * TILE : (j + 1) * TILE].astype(F32)
        down = jnp.transpose(jnp.broadcast_to(here, (TILE, TILE))).astype(jnp.int32)
        dest = down // PAIR
        slot = jnp.where(lanes == down % PAIR, 1.0, 0.0)
        hot = [jnp.where(dest % 8 == i, slot, 0.0).astype(BF16) for i in range(8)]
        found = jnp.dot(
            jnp.concatenate(hot, axis=1),
            jnp.concatenate(
                [back_ref[8 * i : 8 * i + 8].reshape(8 * PAIR, HD) for i in range(CTX // 8)], axis=1
            ),
            preferred_element_type=F32,
        )
        row = found[:, 0:HD]
        for i in range(1, CTX // 8):
            row = jnp.where(dest // 8 == i, found[:, i * HD : (i + 1) * HD], row)
        out_ref[j * TILE : (j + 1) * TILE, :] = row.astype(BF16)


def fetch(target, back, tile=1024):
    tokens = target.shape[1]
    return pl.pallas_call(
        fetch_kernel,
        grid=(tokens // tile,),
        out_shape=jax.ShapeDtypeStruct((tokens, HD), BF16),
        in_specs=[
            pl.BlockSpec((1, tile), lambda s: (0, s)),
            pl.BlockSpec((CTX, PAIR, HD), lambda s: (0, 0, 0)),
        ],
        out_specs=pl.BlockSpec((tile, HD), lambda s: (s, 0)),
        compiler_params=pltpu.CompilerParams(
            dimension_semantics=("arbitrary",), vmem_limit_bytes=32 << 20
        ),
        cost_estimate=pl.CostEstimate(
            flops=2 * tokens * 1024 * 512, bytes_accessed=2 << 20, transcendentals=0
        ),
        name="fetch",
    )(target, back)


def project_kernel(heads_ref, w_ref, out_ref):
    halves, columns = w_ref.shape[0], w_ref.shape[1]
    each = heads_ref.shape[0] // halves
    total = 0.0
    for c in range(halves):
        left = jnp.concatenate([heads_ref[c * each + i] for i in range(each)], axis=1)
        right = jnp.concatenate([w_ref[c, n] for n in range(columns)], axis=1)
        total = total + jnp.dot(left, right, preferred_element_type=F32)
    for n in range(columns):
        out_ref[n] = total[:, n * HD : (n + 1) * HD].astype(BF16)


def project(heads, w_all, columns=2):
    halves, blocks, depth, width = w_all.shape
    tokens = heads.shape[1]
    return pl.pallas_call(
        project_kernel,
        grid=(blocks // columns,),
        out_shape=jax.ShapeDtypeStruct((blocks, tokens, width), BF16),
        in_specs=[
            pl.BlockSpec(heads.shape, lambda s: (0, 0, 0)),
            pl.BlockSpec((halves, columns, depth, width), lambda s: (0, s, 0, 0)),
        ],
        out_specs=pl.BlockSpec((columns, tokens, width), lambda s: (s, 0, 0)),
        compiler_params=pltpu.CompilerParams(
            dimension_semantics=("arbitrary",), vmem_limit_bytes=60 << 20
        ),
        cost_estimate=pl.CostEstimate(
            flops=2 * tokens * halves * depth * blocks * width,
            bytes_accessed=9 << 20,
            transcendentals=0,
        ),
        name="project",
    )(heads, w_all)


def on_device(queries, keys, values, cluster_ids, w_out, old_sums):
    hg_count = lax.axis_size("hg")
    tok_rows = queries.shape[0]
    core = (lax.axis_index("ctx") % 2).astype(jnp.int32).reshape(1)
    outgoing, target, w_half = place(core, cluster_ids[:, :, 0], queries, keys, values, w_out)
    chips = [list(range(2 * hg_count * i, 2 * hg_count * (i + 1))) for i in range(CTX // 2)]
    w_all = lax.all_gather(w_half, ("ctx", "hg"), axis_index_groups=chips)
    slab = lax.all_to_all(outgoing, "ctx", split_axis=0, concat_axis=0, tiled=True)
    mixed_rows, centroid_sums = attend(slab, old_sums[0])
    returned = lax.all_to_all(mixed_rows, "ctx", split_axis=0, concat_axis=0, tiled=True)
    attention = fetch(target, returned).reshape(hg_count, tok_rows // hg_count, HD)
    all_heads = lax.all_to_all(attention, "hg", split_axis=0, concat_axis=0, tiled=True)
    mixed = project(all_heads, w_all.reshape(2, hg_count, -1, w_out.shape[1]))
    projected = lax.all_to_all(mixed, "hg", split_axis=0, concat_axis=0, tiled=True)
    return (projected.reshape(tok_rows, w_out.shape[1]), centroid_sums[None])


def solution(mesh):
    placed = (
        P("ctx", "hg"),
        P("ctx", "hg"),
        P("ctx", "hg"),
        P("hg", "ctx", None),
        P(None, "hg"),
        P("hg", "ctx", None),
    )
    return jax.shard_map(
        on_device,
        mesh=mesh,
        in_specs=placed,
        out_specs=(P("ctx", "hg"), P("hg", "ctx", None)),
        check_vma=False,
    )
```

time: 200 us -> 194 us (0.970)
  the two profiles are of different devices: /device:TPU:2 before, /device:TPU:32 now
where the time goes in v3:
time: 194 us; the launch traced here: 193 us
  blocking collectives  147 us (76%)
  Pallas kernels  30.8 us (16%)
  between operations  14.1 us (7%)
    all_to_all x1, blocking collectives, on_device(): lax.all_to_all(outgoing, 'ctx', split_axis=0, concat_axis=0, tiled=True)  47.1 us
    all_to_all x1, blocking collectives, on_device(): lax.all_to_all(attention, 'hg', split_axis=0, concat_axis=0, tiled=True)  44.1 us
    all_to_all x1, blocking collectives, on_device(): lax.all_to_all(mixed, 'hg', split_axis=0, concat_axis=0, tiled=True)  35.3 us
    all_to_all x1, blocking collectives, on_device(): lax.all_to_all(mixed_rows, 'ctx', split_axis=0, concat_axis=0, tiled=True)  20.7 us
    pallas_call x1, Pallas kernels, place(): pl.pallas_call(place_kernel, grid_spec=pltpu.PrefetchScalarGridSpec(num_s...  13.3 us
    pallas_call x1, Pallas kernels, project(): pl.pallas_call(project_kernel, grid=(blocks // columns,), out_shape=jax.S...  7.86 us
    pallas_call x1, Pallas kernels, attend(): pl.pallas_call(attend_kernel, grid=(LOCAL // count,), out_shape=(jax.Shap...  6.06 us
  transfers between devices with their start and end apart: 1, of which 0 were waited for; matrix products, arithmetic and copies ran while one was open for 0% of the time, Pallas kernels for 5%

profile of v3, /device:TPU:32, one launch (start us, length us, event | category | flops | bytes accessed | tf_op | source)
XLA Modules:
  0.0 193.0 jit_solution(14055924521208548156)
XLA Ops:
  7.2 0.0 all-gather.3.cloned.1.call-start
  7.2 13.3 %place.1 = (bf16[32,3,128,128]{3,2,1,0:T(8,128)(2,1)}, s32[1,2048]{1,0:T(1,128)}, bf16[1024,128]{1,0:T(8,128)(2,1)}) custom-call(s32[1]{0:T(128)} %bitcast.core_ref, s32[1,2048]{1,0:T(1,128)} %bitcast.11, bf16[2048,128]{1,0:T(8,128)(2,1)} %q_ref.1, bf16[2048,128]{1,0:T(8,128)(2,1)} %k_ref.1, bf16[2048,128]{1,0:T(8,128)(2,1)} %v_ref.1, bf16[2048,128]{1,0:T(8,128)(2,1)} %w_ref.1), custom_call_target="tpu_custom_call" | custom-call | flops 8589934592 | bytes 5242880 | tf_op jit(solution)/shard_map/place/pallas_call | solution.py:83
  20.5 0.0 all-gather.3.cloned.1.call-update
  20.5 0.0 copy-start
  20.5 47.1 %all_to_all.20.q_ref.k_ref.v_ref = bf16[32,3,128,128]{3,2,1,0:T(8,128)(2,1)S(1)} all-to-all(bf16[32,3,128,128]{3,2,1,0:T(8,128)(2,1)} %get-tuple-element.8), channel_id=1, replica_groups=mesh['ctx'=32,'hg'=16] {'ctx'}, dimensions={0} | all-to-all | bytes 6291456 | tf_op jit(solution)/shard_map/all_to_all | solution.py:269
  67.7 0.0 copy-done
  67.7 0.0 copy-start.1
  67.7 6.1 %attend.1 = (bf16[32,128,128]{2,1,0:T(8,128)(2,1)S(1)}, f32[16,128]{1,0:T(8,128)}) custom-call(bf16[32,3,128,128]{3,2,1,0:T(8,128)(2,1)S(1)} %all_to_all.20.q_ref.k_ref.v_ref, bf16[32,3,128,128]{3,2,1,0:T(8,128)(2,1)S(1)} %all_to_all.20.q_ref.k_ref.v_ref, bf16[32,3,128,128]{3,2,1,0:T(8,128)(2,1)S(1)} %all_to_all.20.q_ref.k_ref.v_ref, f32[16,128]{1,0:T(8,128)S(1)} %bitcast.8), custom_call_target="tpu_custom_call" | custom-call | flops 536870912 | bytes 5242880 | tf_op jit(solution)/shard_map/attend/pallas_call | solution.py:162
  73.7 20.7 %all_to_all.21.back_ref = bf16[32,128,128]{2,1,0:T(8,128)(2,1)S(1)} all-to-all(bf16[32,128,128]{2,1,0:T(8,128)(2,1)S(1)} %get-tuple-element.9), channel_id=1, replica_groups=mesh['ctx'=32,'hg'=16] {'ctx'}, dimensions={0} | all-to-all | bytes 2097152 | tf_op jit(solution)/shard_map/all_to_all | solution.py:271
  94.4 0.0 copy-done.1
  94.4 3.6 %fetch.1 = bf16[2048,128]{1,0:T(8,128)(2,1)S(1)} custom-call(s32[1,2048]{1,0:T(1,128)S(1)} %copy-done.1, bf16[32,128,128]{2,1,0:T(8,128)(2,1)S(1)} %all_to_all.21.back_ref), custom_call_target="tpu_custom_call" | custom-call | flops 2147483648 | bytes 2097152 | tf_op jit(solution)/shard_map/fetch/pallas_call | solution.py:207
  98.0 44.1 %all_to_all.22.heads_ref = bf16[16,128,128]{2,1,0:T(8,128)(2,1)} all-to-all(bf16[16,128,128]{2,1,0:T(8,128)(2,1)S(1)} %bitcast.7), channel_id=1, replica_groups=mesh['ctx'=32,'hg'=16] {'hg'}, dimensions={0} | all-to-all | bytes 1048576 | tf_op jit(solution)/shard_map/all_to_all | solution.py:273
  142.2 0.0 all-gather.3.cloned.1.call-done
  142.2 7.9 %project.1 = bf16[16,128,128]{2,1,0:T(8,128)(2,1)} custom-call(bf16[16,128,128]{2,1,0:T(8,128)(2,1)} %all_to_all.22.heads_ref, bf16[2,16,1024,128]{3,2,1,0:T(8,128)(2,1)} %bitcast.9), custom_call_target="tpu_custom_call" | custom-call | flops 1073741824 | bytes 9437184 | tf_op jit(solution)/shard_map/project/pallas_call | solution.py:241
  150.0 35.3 %all_to_all.23 = bf16[16,128,128]{2,1,0:T(8,128)(2,1)S(1)} all-to-all(bf16[16,128,128]{2,1,0:T(8,128)(2,1)} %project.1), channel_id=1, replica_groups=mesh['ctx'=32,'hg'=16] {'hg'}, dimensions={0} | all-to-all | bytes 1048576 | tf_op jit(solution)/shard_map/all_to_all | solution.py:275
  185.3 0.8 copy.9
Async XLA Ops:
  7.2 135.0 %all-gather.3.cloned.1.call-start = ((), (), s32[]{:S(2)}) async-start(), calls=%async_computation.4 | async-start | bytes 8650752 | tf_op jit(solution)/shard_map/all_gather | solution.py:268
  20.5 47.1 %copy-start = (f32[1,16,128]{2,1,0:T(8,128)S(1)}, f32[1,16,128]{2,1,0:T(8,128)}, u32[]{:S(2)}) copy-start(f32[1,16,128]{2,1,0:T(8,128)} %param.11) | copy-start | bytes 24580
  67.7 26.8 %copy-start.1 = (s32[1,2048]{1,0:T(1,128)S(1)}, s32[1,2048]{1,0:T(1,128)}, u32[]{:S(2)}) copy-start(s32[1,2048]{1,0:T(1,128)} %get-tuple-element.7.target_ref) | copy-start | bytes 24580
Sparse Core Ops, SparseCore 0:
  20.6 83.5 all-gather.2

commit v4 on v3

--- a/solution.py
+++ b/solution.py
@@ -1,3 +1,5 @@
+import functools
+
 import jax
 import jax.numpy as jnp
 from jax import lax
@@ -11,6 +13,10 @@
 CTX = 32
 LOCAL = NCL // CTX
 PAIR = LOCAL * SLOTS
+ROOM = 96
+META = 8
+CHUNK = 3 * ROOM + META
+NO_ROW = 255.0
 TILE = 128
 
 DECAY = 0.9
@@ -23,10 +29,26 @@
 BF16 = jnp.bfloat16
 
 
+def ranks_of(ids):
+    wide = ids.astype(F32)
+    before = lax.broadcasted_iota(jnp.int32, (TILE, TILE), 0) < lax.broadcasted_iota(
+        jnp.int32, (TILE, TILE), 1
+    )
+    columns = [wide[:, i * TILE : (i + 1) * TILE] for i in range(ids.shape[1] // TILE)]
+    down = [jnp.transpose(jnp.broadcast_to(c, (TILE, TILE))) for c in columns]
+    ranks = []
+    for j, column in enumerate(columns):
+        here = jnp.broadcast_to(column, (TILE, TILE))
+        same = jnp.where((down[j] == here) & before, 1.0, 0.0)
+        for i in range(j):
+            same = same + jnp.where(down[i] == here, 1.0, 0.0)
+        ranks.append(jnp.sum(same, axis=0, keepdims=True))
+    return jnp.concatenate(ranks, axis=1).astype(jnp.int32), down
+
+
 def place_kernel(
-    core_ref, ids_ref, q_ref, k_ref, v_ref, w_ref, out_ref, target_ref, half_ref, rows, slot_hot, hot, dest_row
+    ids_ref, q_ref, k_ref, v_ref, out_ref, target_ref, rows, slot_hot, hot, dest_row
 ):
-    del core_ref
     step = pl.program_id(0)
     per_step = out_ref.shape[0]
     tokens = ids_ref.shape[1]
@@ -34,22 +56,8 @@
     @pl.when(step == 0)
     def _():
         ids = ids_ref[...]
-        wide = ids.astype(F32)
-        before = lax.broadcasted_iota(jnp.int32, (TILE, TILE), 0) < lax.broadcasted_iota(
-            jnp.int32, (TILE, TILE), 1
-        )
-        columns = [wide[:, i * TILE : (i + 1) * TILE] for i in range(tokens // TILE)]
-        down = [jnp.transpose(jnp.broadcast_to(c, (TILE, TILE))) for c in columns]
-        ranks = []
-        for j, column in enumerate(columns):
-            here = jnp.broadcast_to(column, (TILE, TILE))
-            same = jnp.where((down[j] == here) & before, 1.0, 0.0)
-            for i in range(j):
-                same = same + jnp.where(down[i] == here, 1.0, 0.0)
-            ranks.append(jnp.sum(same, axis=0, keepdims=True))
-        rank = jnp.concatenate(ranks, axis=1).astype(jnp.int32)
+        rank, _ = ranks_of(ids)
         target_ref[...] = ids * SLOTS + rank
-        half_ref[...] = w_ref[...]
         slot = (ids % LOCAL) * SLOTS + rank
         slots = lax.broadcasted_iota(jnp.int32, (PAIR, tokens), 0)
         slot_hot[...] = jnp.where(slots == slot, 1.0, 0.0).astype(BF16)
@@ -75,27 +83,24 @@
     out_ref[:, 2] = others[:, HD : 2 * HD].astype(BF16).reshape(shape)
 
 
-def place(core, ids_row, queries, keys, values, w_out, per_step=8):
+def place(ids_row, queries, keys, values, per_step=8):
     tokens = queries.shape[0]
-    half = w_out.shape[0] // 2
-    whole = pl.BlockSpec((tokens, HD), lambda s, c: (0, 0))
-    line = pl.BlockSpec((1, tokens), lambda s, c: (0, 0))
+    whole = pl.BlockSpec((tokens, HD), lambda s: (0, 0))
+    line = pl.BlockSpec((1, tokens), lambda s: (0, 0))
     return pl.pallas_call(
         place_kernel,
         grid_spec=pltpu.PrefetchScalarGridSpec(
-            num_scalar_prefetch=1,
+            num_scalar_prefetch=0,
             grid=(CTX // per_step,),
             in_specs=[
                 line,
                 whole,
                 whole,
                 whole,
-                pl.BlockSpec((half, w_out.shape[1]), lambda s, c: (c[0], 0)),
             ],
             out_specs=(
-                pl.BlockSpec((per_step, 3, PAIR, HD), lambda s, c: (s, 0, 0, 0)),
+                pl.BlockSpec((per_step, 3, PAIR, HD), lambda s: (s, 0, 0, 0)),
                 line,
-                pl.BlockSpec((half, w_out.shape[1]), lambda s, c: (0, 0)),
             ),
             scratch_shapes=[
                 pltpu.VMEM((tokens, 4 * HD), BF16),
@@ -107,7 +112,6 @@
         out_shape=(
             jax.ShapeDtypeStruct((CTX, 3, PAIR, HD), BF16),
             jax.ShapeDtypeStruct((1, tokens), jnp.int32),
-            jax.ShapeDtypeStruct((half, w_out.shape[1]), BF16),
         ),
         compiler_params=pltpu.CompilerParams(
             dimension_semantics=("arbitrary",), vmem_limit_bytes=60 << 20
@@ -116,7 +120,7 @@
             flops=2 * NCL * SLOTS * tokens * 4 * HD, bytes_accessed=5 << 20, transcendentals=0
         ),
         name="place",
-    )(core, ids_row, queries, keys, values, w_out)
+    )(ids_row, queries, keys, values)
 
 
 def attend_kernel(q_ref, k_ref, v_ref, old_ref, out_ref, sums_ref):
@@ -223,33 +227,282 @@
     )(target, back)
 
 
-def project_kernel(heads_ref, w_ref, out_ref):
-    halves, columns = w_ref.shape[0], w_ref.shape[1]
+def pack_kernel(
+    ids_ref, q_ref, k_ref, v_ref,
+    out_ref, dest_ref, at_ref,
+    held, rows, row_hot, hot, slot_rows, over, done,
+):
+    step = pl.program_id(0)
+    folds, per_step = out_ref.shape[0], out_ref.shape[1]
+    tokens = ids_ref.shape[1]
+    fold = CTX // folds
+
+    @pl.when(step == 0)
+    def _():
+        copies = [
+            pltpu.make_async_copy(ref, held.at[i], done.at[i])
+            for i, ref in enumerate((q_ref, k_ref, v_ref))
+        ]
+        for copy in copies:
+            copy.start()
+        ids = ids_ref[...]
+        rank, down = ranks_of(ids)
+        dest, near = ids // LOCAL, ids % LOCAL
+        dest_ref[...] = dest
+        slots = lax.broadcasted_iota(jnp.int32, (PAIR, tokens), 0)
+        group = slots // SLOTS
+        to_dest = lax.broadcasted_iota(jnp.int32, (CTX, tokens), 0) == dest
+        to_dest = jnp.where(to_dest, 1.0, 0.0).astype(BF16)
+        equal = jnp.where(near == group, 1.0, 0.0).astype(BF16)
+        less = jnp.where(near < group, 1.0, 0.0).astype(BF16)
+        dims = (((1,), (1,)), ((), ()))
+        count = lax.dot_general(to_dest, equal, dims, preferred_element_type=F32)
+        start = lax.dot_general(to_dest, less, dims, preferred_element_type=F32)
+        start_down = lax.dot_general(less, to_dest, dims, preferred_element_type=F32)
+        first = jnp.dot(start_down.astype(BF16), to_dest, preferred_element_type=F32)
+        first = jnp.sum(jnp.where(slots == near * SLOTS, first, 0.0), axis=0, keepdims=True)
+        at = first.astype(jnp.int32) + rank
+        at_ref[...] = at
+        slot = lax.broadcasted_iota(jnp.int32, (CTX, PAIR), 1) % SLOTS
+        slot = slot.astype(F32)
+        slot_rows[...] = jnp.where(slot < count, start + slot, NO_ROW)
+        most = jnp.max(start + count, axis=0, keepdims=True)
+        most = jnp.max(most, axis=1, keepdims=True)
+        over[...] = jnp.broadcast_to(jnp.where(most > ROOM, 1.0, 0.0), over.shape)
+        index = lax.broadcasted_iota(jnp.int32, (ROOM, tokens), 0)
+        row_hot[...] = jnp.where(index == at, 1.0, 0.0).astype(BF16)
+        inside = []
+        for column in down:
+            parts = [
+                (column >= f * fold * LOCAL) & (column < (f + 1) * fold * LOCAL)
+                for f in range(folds)
+            ]
+            inside.append([jnp.where(part, 1.0, 0.0).astype(BF16) for part in parts])
+        for i, copy in enumerate(copies):
+            copy.wait()
+            for j, parts in enumerate(inside):
+                block = held[i, j * TILE : (j + 1) * TILE, :]
+                for f, part in enumerate(parts):
+                    low = (3 * f + i) * HD
+                    rows[j * TILE : (j + 1) * TILE, low : low + HD] = block * part
+
+    for i in range(per_step):
+        mine = jnp.where(dest_ref[...] % fold == step * per_step + i, 1.0, 0.0)
+        mine = jnp.broadcast_to(mine, (16, tokens)).astype(BF16)
+        here = row_hot[...].reshape(ROOM // 16, 16, tokens) * mine[None]
+        hot[i * ROOM : (i + 1) * ROOM, :] = here.reshape(ROOM, tokens)
+    placed = jnp.dot(hot[...], rows[...], preferred_element_type=F32).astype(BF16)
+    line = lax.broadcasted_iota(jnp.int32, (META, HD), 0)
+    for f in range(folds):
+        for part in range(3):
+            low = (3 * f + part) * HD
+            columns = placed[:, low : low + HD].reshape(per_step, ROOM, HD)
+            out_ref[f, :, part * ROOM : (part + 1) * ROOM] = columns
+        for i in range(per_step):
+            mine = slot_rows[pl.ds(f * fold + step * per_step + i, 1), :]
+            meta = jnp.where(line == 0, mine, jnp.where(line == 1, over[...], 0.0))
+            out_ref[f, i, 3 * ROOM :] = meta.astype(BF16)
+
+
+def pack(ids_row, queries, keys, values, per_step=8, folds=2):
+    tokens = queries.shape[0]
+    line = pl.BlockSpec((1, tokens), lambda s: (0, 0))
+    anywhere = pl.BlockSpec(memory_space=pl.ANY)
+    outgoing, dest, at = pl.pallas_call(
+        pack_kernel,
+        grid=(CTX // folds // per_step,),
+        out_shape=(
+            jax.ShapeDtypeStruct((folds, CTX // folds, CHUNK, HD), BF16),
+            jax.ShapeDtypeStruct((1, tokens), jnp.int32),
+            jax.ShapeDtypeStruct((1, tokens), jnp.int32),
+        ),
+        in_specs=[line, anywhere, anywhere, anywhere],
+        out_specs=(
+            pl.BlockSpec((folds, per_step, CHUNK, HD), lambda s: (0, s, 0, 0)),
+            line,
+            line,
+        ),
+        scratch_shapes=[
+            pltpu.VMEM((3, tokens, HD), BF16),
+            pltpu.VMEM((tokens, 3 * folds * HD), BF16),
+            pltpu.VMEM((ROOM, tokens), BF16),
+            pltpu.VMEM((per_step * ROOM, tokens), BF16),
+            pltpu.VMEM((CTX, PAIR), F32),
+            pltpu.VMEM((META, HD), F32),
+            pltpu.SemaphoreType.DMA((3,)),
+        ],
+        compiler_params=pltpu.CompilerParams(
+            dimension_semantics=("arbitrary",), vmem_limit_bytes=60 << 20
+        ),
+        cost_estimate=pl.CostEstimate(
+            flops=2 * CTX * ROOM * tokens * 3 * HD, bytes_accessed=5 << 20, transcendentals=0
+        ),
+        name="pack",
+    )(ids_row, queries, keys, values)
+    return outgoing.reshape(CTX, CHUNK, HD), dest, at
+
+
+def mix_kernel(recv_ref, old_ref, out_ref, sums_ref, over_ref, wide, mixed, total):
+    sources = recv_ref.shape[0]
+    members = sources * SLOTS
+    lanes = lax.broadcasted_iota(jnp.int32, (PAIR, HD), 1).astype(F32)
+    index = lax.broadcasted_iota(jnp.int32, (ROOM, PAIR), 0).astype(F32)
+    first_lane = (lax.broadcasted_iota(jnp.int32, (16, HD), 1) == 0).astype(BF16)
+    ones = jnp.ones((members, HD), BF16)
+    dims = (((1,), (1,)), ((), ()))
+
+    flags = jnp.max(recv_ref[:, 3 * ROOM :, :].astype(F32), axis=0)
+    over_ref[0, 0] = jnp.max(flags[1:2, :]).astype(jnp.int32)
+
+    def slot_row(source):
+        return recv_ref[source, 3 * ROOM :, :].astype(F32)[0:1, :]
+
+    def expand(source):
+        down = jnp.transpose(jnp.broadcast_to(slot_row(source), (PAIR, PAIR)))
+        take = jnp.where(down == lanes, 1.0, 0.0).astype(BF16)[:, 0:ROOM]
+        parts = [recv_ref[source, i * ROOM : (i + 1) * ROOM, :] for i in range(3)]
+        found = jnp.dot(take, jnp.concatenate(parts, axis=1), preferred_element_type=F32)
+        mark = jnp.where((down == NO_ROW) & (lanes == 0.0), EMPTY, 0.0)
+        keys = found[:, HD : 2 * HD]
+        total[...] += keys
+        wide[0, :, source] = found[:, 0:HD].reshape(LOCAL, SLOTS, HD)
+        wide[1, :, source] = (keys + mark).reshape(LOCAL, SLOTS, HD)
+        wide[2, :, source] = found[:, 2 * HD :].reshape(LOCAL, SLOTS, HD)
+
+    def attend_one(cluster):
+        q, k, v = (wide[i, cluster].reshape(members, HD).astype(BF16) for i in range(3))
+        both = jnp.concatenate([q, first_lane], axis=0)
+        both = lax.dot_general(both, k, dims, preferred_element_type=F32)
+        present = both[members : members + 1] < 0.5 * EMPTY
+        scores = jnp.where(present, both[0:members], NEG_FILL)
+        weights = jnp.exp2((scores - jnp.max(scores, axis=1, keepdims=True)) * EXP2_SCALE)
+        totals = jnp.dot(
+            weights.astype(BF16), jnp.concatenate([v, ones], axis=1), preferred_element_type=F32
+        )
+        mixed[:, cluster] = (totals[:, 0:HD] / totals[:, HD:]).reshape(sources, SLOTS, HD)
+
+    def compress(source):
+        put = jnp.where(index == slot_row(source), 1.0, 0.0).astype(BF16)
+        slots = mixed[source].reshape(PAIR, HD).astype(BF16)
+        out_ref[source] = jnp.dot(put, slots, preferred_element_type=F32).astype(BF16)
+
+    def each(body, count, unroll):
+        def some(step, carry):
+            for i in range(unroll):
+                body(step * unroll + i)
+            return carry
+
+        lax.fori_loop(0, count // unroll, some, 0)
+
+    total[...] = jnp.zeros_like(total)
+    each(expand, sources, sources)
+    member_sums = jnp.sum(total[...].reshape(LOCAL, SLOTS, HD), axis=1)
+    sums_ref[...] = DECAY * old_ref[...] + (1.0 - DECAY) * member_sums
+    each(attend_one, LOCAL, LOCAL)
+    each(compress, sources, sources)
+
+
+def mix(recv, old_sums):
+    return pl.pallas_call(
+        mix_kernel,
+        out_shape=(
+            jax.ShapeDtypeStruct((CTX, ROOM, HD), BF16),
+            jax.ShapeDtypeStruct((LOCAL, HD), F32),
+            jax.ShapeDtypeStruct((1, 1), jnp.int32),
+        ),
+        in_specs=[pl.BlockSpec(memory_space=pltpu.VMEM)] * 2,
+        out_specs=(
+            pl.BlockSpec(memory_space=pltpu.VMEM),
+            pl.BlockSpec(memory_space=pltpu.VMEM),
+            pl.BlockSpec(memory_space=pltpu.SMEM),
+        ),
+        scratch_shapes=[
+            pltpu.VMEM((3, LOCAL, CTX, SLOTS, HD), F32),
+            pltpu.VMEM((CTX, LOCAL, SLOTS, HD), F32),
+            pltpu.VMEM((PAIR, HD), F32),
+        ],
+        compiler_params=pltpu.CompilerParams(vmem_limit_bytes=32 << 20),
+        cost_estimate=pl.CostEstimate(
+            flops=4 * LOCAL * 256 * 256 * HD,
+            bytes_accessed=5 << 20,
+            transcendentals=LOCAL * 256 * 256,
+        ),
+        name="mix",
+    )(recv, old_sums)
+
+
+def unpack_kernel(dest_ref, at_ref, back_ref, out_ref, table):
+    tokens = out_ref.shape[0]
+
+    @pl.when(pl.program_id(0) == 0)
+    def _():
+        for i in range(CTX):
+            low, high = (i % 8) * PAIR, i // 8 * HD
+            table[low : low + ROOM, high : high + HD] = back_ref[i]
+            table[low + ROOM : low + PAIR, high : high + HD] = jnp.zeros((PAIR - ROOM, HD), BF16)
+
+    lanes = lax.broadcasted_iota(jnp.int32, (TILE, PAIR), 1)
+
+    def down(ref, j):
+        here = ref[:, j * TILE : (j + 1) * TILE].astype(F32)
+        return jnp.transpose(jnp.broadcast_to(here, (TILE, TILE))).astype(jnp.int32)
+
+    for j in range(tokens // TILE):
+        dest = down(dest_ref, j)
+        slot = jnp.where(lanes == down(at_ref, j), 1.0, 0.0)
+        hot = [jnp.where(dest % 8 == i, slot, 0.0).astype(BF16) for i in range(8)]
+        found = jnp.dot(jnp.concatenate(hot, axis=1), table[...], preferred_element_type=F32)
+        row = found[:, 0:HD]
+        for i in range(1, CTX // 8):
+            row = jnp.where(dest // 8 == i, found[:, i * HD : (i + 1) * HD], row)
+        out_ref[j * TILE : (j + 1) * TILE, :] = row.astype(BF16)
+
+
+def unpack(dest, at, back, tile=1024):
+    tokens = dest.shape[1]
+    line = pl.BlockSpec((1, tile), lambda s: (0, s))
+    return pl.pallas_call(
+        unpack_kernel,
+        grid=(tokens // tile,),
+        out_shape=jax.ShapeDtypeStruct((tokens, HD), BF16),
+        in_specs=[line, line, pl.BlockSpec((CTX, ROOM, HD), lambda s: (0, 0, 0))],
+        out_specs=pl.BlockSpec((tile, HD), lambda s: (s, 0)),
+        scratch_shapes=[pltpu.VMEM((8 * PAIR, CTX // 8 * HD), BF16)],
+        compiler_params=pltpu.CompilerParams(
+            dimension_semantics=("arbitrary",), vmem_limit_bytes=32 << 20
+        ),
+        cost_estimate=pl.CostEstimate(
+            flops=2 * tokens * 1024 * 512, bytes_accessed=2 << 20, transcendentals=0
+        ),
+        name="unpack",
+    )(dest, at, back)
+
+
+def project_kernel(heads_ref, w_ref, out_ref, *, columns):
+    halves, blocks = w_ref.shape[0], w_ref.shape[1]
     each = heads_ref.shape[0] // halves
-    total = 0.0
-    for c in range(halves):
-        left = jnp.concatenate([heads_ref[c * each + i] for i in range(each)], axis=1)
-        right = jnp.concatenate([w_ref[c, n] for n in range(columns)], axis=1)
-        total = total + jnp.dot(left, right, preferred_element_type=F32)
-    for n in range(columns):
-        out_ref[n] = total[:, n * HD : (n + 1) * HD].astype(BF16)
-
-
-def project(heads, w_all, columns=2):
+    left = [
+        jnp.concatenate([heads_ref[c * each + i] for i in range(each)], axis=1)
+        for c in range(halves)
+    ]
+    for low in range(0, blocks, columns):
+        total = 0.0
+        for c in range(halves):
+            right = jnp.concatenate([w_ref[c, low + n] for n in range(columns)], axis=1)
+            total = total + jnp.dot(left[c], right, preferred_element_type=F32)
+        for n in range(columns):
+            out_ref[low + n] = total[:, n * HD : (n + 1) * HD].astype(BF16)
+
+
+def project(heads, w_all, columns=4):
     halves, blocks, depth, width = w_all.shape
     tokens = heads.shape[1]
     return pl.pallas_call(
-        project_kernel,
-        grid=(blocks // columns,),
+        functools.partial(project_kernel, columns=columns),
         out_shape=jax.ShapeDtypeStruct((blocks, tokens, width), BF16),
-        in_specs=[
-            pl.BlockSpec(heads.shape, lambda s: (0, 0, 0)),
-            pl.BlockSpec((halves, columns, depth, width), lambda s: (0, s, 0, 0)),
-        ],
-        out_specs=pl.BlockSpec((columns, tokens, width), lambda s: (s, 0, 0)),
-        compiler_params=pltpu.CompilerParams(
-            dimension_semantics=("arbitrary",), vmem_limit_bytes=60 << 20
-        ),
+        in_specs=[pl.BlockSpec(memory_space=pltpu.VMEM)] * 2,
+        out_specs=pl.BlockSpec(memory_space=pltpu.VMEM),
+        compiler_params=pltpu.CompilerParams(vmem_limit_bytes=32 << 20),
         cost_estimate=pl.CostEstimate(
             flops=2 * tokens * halves * depth * blocks * width,
             bytes_accessed=9 << 20,
@@ -259,19 +512,34 @@
     )(heads, w_all)
 
 
+def over_ctx(chunks):
+    return lax.all_to_all(chunks, "ctx", split_axis=0, concat_axis=0, tiled=True)
+
+
 def on_device(queries, keys, values, cluster_ids, w_out, old_sums):
     hg_count = lax.axis_size("hg")
     tok_rows = queries.shape[0]
-    core = (lax.axis_index("ctx") % 2).astype(jnp.int32).reshape(1)
-    outgoing, target, w_half = place(core, cluster_ids[:, :, 0], queries, keys, values, w_out)
+    half = w_out.shape[0] // 2
+    w_half = lax.dynamic_slice_in_dim(w_out, lax.axis_index("ctx") % 2 * half, half)
+    ids_row = cluster_ids[:, :, 0]
+    outgoing, dest, at = pack(ids_row, queries, keys, values)
     chips = [list(range(2 * hg_count * i, 2 * hg_count * (i + 1))) for i in range(CTX // 2)]
     w_all = lax.all_gather(w_half, ("ctx", "hg"), axis_index_groups=chips)
-    slab = lax.all_to_all(outgoing, "ctx", split_axis=0, concat_axis=0, tiled=True)
-    mixed_rows, centroid_sums = attend(slab, old_sums[0])
-    returned = lax.all_to_all(mixed_rows, "ctx", split_axis=0, concat_axis=0, tiled=True)
-    attention = fetch(target, returned).reshape(hg_count, tok_rows // hg_count, HD)
+    mixed_rows, sums, over = mix(over_ctx(outgoing), old_sums[0])
+
+    def compact():
+        return unpack(dest, at, over_ctx(mixed_rows)), sums
+
+    def general():
+        slots, target = place(ids_row, queries, keys, values)
+        slot_rows, slot_sums = attend(over_ctx(slots), old_sums[0])
+        return fetch(target, over_ctx(slot_rows)), slot_sums
+
+    attention, centroid_sums = lax.cond(over[0, 0] > 0, general, compact)
+    attention = attention.reshape(hg_count, tok_rows // hg_count, HD)
     all_heads = lax.all_to_all(attention, "hg", split_axis=0, concat_axis=0, tiled=True)
-    mixed = project(all_heads, w_all.reshape(2, hg_count, -1, w_out.shape[1]))
+    w_all = w_all.reshape(2, hg_count, -1, w_out.shape[1])
+    mixed = project(all_heads, w_all)
     projected = lax.all_to_all(mixed, "hg", split_axis=0, concat_axis=0, tiled=True)
     return (projected.reshape(tok_rows, w_out.shape[1]), centroid_sums[None])
 

time: 194 us -> 180 us (0.928)
  the two profiles are of different devices: /device:TPU:32 before, /device:TPU:2 now
where the time goes in v4:
time: 180 us; the launch traced here: 179 us
  blocking collectives  96.2 us (53%)
  waiting for transfers between devices  31.7 us (18%)
  Pallas kernels  20.8 us (12%)
  between operations  14.8 us (8%)
  starting transfers between devices  9.81 us (5%)
  local copies, waits for them, and re-layouts  5.89 us (3%)
    all_to_all x1, blocking collectives, on_device(): lax.all_to_all(attention, 'hg', split_axis=0, concat_axis=0, tiled=True)  42.2 us
    all_to_all x1, blocking collectives, on_device(): lax.all_to_all(mixed, 'hg', split_axis=0, concat_axis=0, tiled=True)  35.5 us
    all_to_all x1, waiting for transfers between devices, over_ctx(): lax.all_to_all(chunks, 'ctx', split_axis=0, concat_axis=0, tiled=True)  31.7 us
    all_to_all x1, blocking collectives, over_ctx(): lax.all_to_all(chunks, 'ctx', split_axis=0, concat_axis=0, tiled=True)  18.5 us
    all_to_all x1, starting transfers between devices, over_ctx(): lax.all_to_all(chunks, 'ctx', split_axis=0, concat_axis=0, tiled=True)  9.77 us
    pallas_call x1, Pallas kernels, pack(): pl.pallas_call(pack_kernel, grid=(CTX // folds // per_step,), out_shape=(...  9.5 us
    pallas_call x1, Pallas kernels, mix(): pl.pallas_call(mix_kernel, out_shape=(jax.ShapeDtypeStruct((CTX, ROOM, HD...  6.81 us
    unnamed x11, local copies, waits for them, and re-layouts  5.17 us
  transfers between devices with their start and end apart: 2, of which 1 were waited for; matrix products, arithmetic and copies ran while one was open for 0% of the time, Pallas kernels for 11%

profile of v4, /device:TPU:2, one launch (start us, length us, event | category | flops | bytes accessed | tf_op | source)
XLA Modules:
  0.0 179.4 jit_solution(4071959216261506576)
XLA Ops:
  7.2 0.0 copy-start
  7.2 0.0 all-gather.3.cloned.1.call-start
  7.2 1.0 copy-done
  8.2 0.7 constant_dynamic-slice_fusion
  8.9 0.0 all-gather.3.cloned.1.call-update
  9.0 9.5 %pack.1 = (bf16[2,16,296,128]{3,2,1,0:T(8,128)(2,1)}, s32[1,2048]{1,0:T(1,128)S(1)}, s32[1,2048]{1,0:T(1,128)S(1)}) custom-call(s32[1,2048]{1,0:T(1,128)} %bitcast.15, bf16[2048,128]{1,0:T(8,128)(2,1)} %q_ref.1, bf16[2048,128]{1,0:T(8,128)(2,1)} %k_ref.1, bf16[2048,128]{1,0:T(8,128)(2,1)} %v_ref.1), custom_call_target="tpu_custom_call" | custom-call | flops 4831838208 | bytes 5242880 | tf_op jit(solution)/shard_map/pack/pallas_call | solution.py:311
  18.5 0.0 copy-start.3
  18.5 0.0 copy-start.4
  18.5 0.0 copy-start.5
  18.5 9.8 %all-to-all-start.3 = ((bf16[32,296,128]{2,1,0:T(8,128)(2,1)}), bf16[32,296,128]{2,1,0:T(8,128)(2,1)S(1)}, u32[]{:S(2)}, u32[]{:S(2)}) async-start(bf16[32,296,128]{2,1,0:T(8,128)(2,1)} %bitcast.10), calls=%async_computation.3 | async-start | bytes 4849664 | tf_op jit(solution)/shard_map/all_to_all | solution.py:516
  28.3 31.7 %all-to-all-done.3.recv_ref = bf16[32,296,128]{2,1,0:T(8,128)(2,1)S(1)} async-done(((bf16[32,296,128]{2,1,0:T(8,128)(2,1)}), bf16[32,296,128]{2,1,0:T(8,128)(2,1)S(1)}, u32[]{:S(2)}, u32[]{:S(2)}) %all-to-all-start.3) | async-done | bytes 2424864 | tf_op jit(solution)/shard_map/all_to_all | solution.py:516
  60.0 0.0 copy-done.3
  60.0 6.8 %mix.1 = (bf16[32,96,128]{2,1,0:T(8,128)(2,1)S(1)}, f32[16,128]{1,0:T(8,128)}, s32[1,1]{1,0:T(1,128)}) custom-call(bf16[32,296,128]{2,1,0:T(8,128)(2,1)S(1)} %all-to-all-done.3.recv_ref, f32[16,128]{1,0:T(8,128)S(1)} %bitcast.13), custom_call_target="tpu_custom_call" | custom-call | flops 536870912 | bytes 5242880 | tf_op jit(solution)/shard_map/mix/pallas_call | solution.py:406
  67.4 0.0 copy-done.4
  67.5 0.0 copy-done.5
  67.5 21.9 %conditional.1 = (bf16[2048,128]{1,0:T(8,128)(2,1)S(1)}, f32[16,128]{1,0:T(8,128)}) conditional(s32[]{:T(128)} %bitcast.4, (bf16[32,96,128]{2,1,0:T(8,128)(2,1)S(1)}, s32[1,2048]{1,0:T(1,128)S(1)}, s32[1,2048]{1,0:T(1,128)S(1)}, f32[16,128]{1,0:T(8,128)}) %tuple.16, (s32[1,2048]{1,0:T(1,128)S(1)}, bf16[2048,128]{1,0:T(8,128)(2,1)S(1)}, ...), branch_computations={%region_0.1_spmd, %region_1.2_spmd} | conditional | flops 11274289152 | bytes 21004332 | solution.py:538
  67.5 18.5 %all_to_all.27.back_ref = bf16[32,96,128]{2,1,0:T(8,128)(2,1)S(1)} all-to-all(bf16[32,96,128]{2,1,0:T(8,128)(2,1)S(1)} %get-tuple-element.20), channel_id=1, replica_groups=mesh['ctx'=32,'hg'=16] {'ctx'}, dimensions={0} | all-to-all | bytes 1572864 | tf_op jit(solution)/shard_map/cond/branch_0_fun/all_to_all | solution.py:516
  86.0 3.2 %unpack.1 = bf16[2048,128]{1,0:T(8,128)(2,1)S(1)} custom-call(s32[1,2048]{1,0:T(1,128)S(1)} %get-tuple-element.18.dest_ref, s32[1,2048]{1,0:T(1,128)S(1)} %get-tuple-element.19.at_ref, bf16[32,96,128]{2,1,0:T(8,128)(2,1)S(1)} %all_to_all.27.back_ref), custom_call_target="tpu_custom_call" | custom-call | flops 2147483648 | bytes 2097152 | tf_op jit(solution)/shard_map/cond/branch_0_fun/unpack/pallas_call | solution.py:464
  89.4 42.2 %all_to_all.30.heads_ref = bf16[16,128,128]{2,1,0:T(8,128)(2,1)S(1)} all-to-all(bf16[16,128,128]{2,1,0:T(8,128)(2,1)S(1)} %bitcast.12), channel_id=1, replica_groups=mesh['ctx'=32,'hg'=16] {'hg'}, dimensions={0} | all-to-all | bytes 1048576 | tf_op jit(solution)/shard_map/all_to_all | solution.py:540
  131.6 0.0 all-gather.3.cloned.1.call-done
  131.6 0.0 copy-start.1
  131.6 3.4 %copy-done.1 = bf16[32768,128]{1,0:T(8,128)(2,1)S(1)} copy-done((bf16[32768,128]{1,0:T(8,128)(2,1)S(1)}, bf16[32768,128]{1,0:T(8,128)(2,1)}, u32[]{:S(2)}) %copy-start.1) | copy-done | bytes 8388632
  134.9 1.3 project.1
  136.2 35.5 %all_to_all.31 = bf16[16,128,128]{2,1,0:T(8,128)(2,1)S(1)} all-to-all(bf16[16,128,128]{2,1,0:T(8,128)(2,1)S(1)} %project.1), channel_id=1, replica_groups=mesh['ctx'=32,'hg'=16] {'hg'}, dimensions={0} | all-to-all | bytes 1048576 | tf_op jit(solution)/shard_map/all_to_all | solution.py:543
  171.7 0.8 copy.13
Async XLA Ops:
  7.2 1.0 copy-start
  7.2 124.4 %all-gather.3.cloned.1.call-start = ((), (), s32[]{:S(2)}) async-start(), calls=%async_computation.6 | async-start | bytes 8650752 | tf_op jit(solution)/shard_map/all_gather | solution.py:527
  18.5 41.5 %copy-start.3 = (f32[1,16,128]{2,1,0:T(8,128)S(1)}, f32[1,16,128]{2,1,0:T(8,128)}, u32[]{:S(2)}) copy-start(f32[1,16,128]{2,1,0:T(8,128)} %param.13) | copy-start | bytes 24580
  18.5 49.0 %copy-start.4 = (bf16[2048,128]{1,0:T(8,128)(2,1)S(1)}, bf16[2048,128]{1,0:T(8,128)(2,1)}, u32[]{:S(2)}) copy-start(bf16[2048,128]{1,0:T(8,128)(2,1)} %q_ref.1) | copy-start | bytes 1572868
  18.5 49.0 %copy-start.5 = (s32[1,2048,1]{1,2,0:T(1,128)S(1)}, s32[1,2048,1]{1,2,0:T(1,128)}, u32[]{:S(2)}) copy-start(s32[1,2048,1]{1,2,0:T(1,128)} %param.11) | copy-start | bytes 24580
  18.5 41.5 %all-to-all-start.3 = ((bf16[32,296,128]{2,1,0:T(8,128)(2,1)}), bf16[32,296,128]{2,1,0:T(8,128)(2,1)S(1)}, u32[]{:S(2)}, u32[]{:S(2)}) async-start(bf16[32,296,128]{2,1,0:T(8,128)(2,1)} %bitcast.10), calls=%async_computation.3 | async-start | bytes 4849664 | tf_op jit(solution)/shard_map/all_to_all | solution.py:516
  131.6 3.4 %copy-start.1 = (bf16[32768,128]{1,0:T(8,128)(2,1)S(1)}, bf16[32768,128]{1,0:T(8,128)(2,1)}, u32[]{:S(2)}) copy-start(bf16[32768,128]{1,0:T(8,128)(2,1)} %all-gather.3.cloned.1.call-done) | copy-start | bytes 25165828
Sparse Core Ops, SparseCore 0:
  10.7 83.6 all-gather.2

commit v5 on v4

--- a/solution.py
+++ b/solution.py
@@ -1,5 +1,3 @@
-import functools
-
 import jax
 import jax.numpy as jnp
 from jax import lax
@@ -17,6 +15,7 @@
 META = 8
 CHUNK = 3 * ROOM + META
 NO_ROW = 255.0
+KEPT = 4
 TILE = 128
 
 DECAY = 0.9
@@ -229,117 +228,119 @@
 
 def pack_kernel(
     ids_ref, q_ref, k_ref, v_ref,
-    out_ref, dest_ref, at_ref,
-    held, rows, row_hot, hot, slot_rows, over, done,
+    sent_ref, code_ref,
+    held, rows, row_hot, hot, slot_rows, out_ref, done, gone,
 ):
-    step = pl.program_id(0)
-    folds, per_step = out_ref.shape[0], out_ref.shape[1]
+    folds = out_ref.shape[0]
     tokens = ids_ref.shape[1]
     fold = CTX // folds
-
-    @pl.when(step == 0)
-    def _():
-        copies = [
-            pltpu.make_async_copy(ref, held.at[i], done.at[i])
-            for i, ref in enumerate((q_ref, k_ref, v_ref))
+    per_step = hot.shape[0] // ROOM
+    copies = [
+        pltpu.make_async_copy(ref, held.at[i], done.at[i])
+        for i, ref in enumerate((q_ref, k_ref, v_ref))
+    ]
+    for copy in copies:
+        copy.start()
+    ids = ids_ref[...]
+    rank, down = ranks_of(ids)
+    dest, near = lax.shift_right_logical(ids, LOCAL.bit_length() - 1), ids & (LOCAL - 1)
+    slots = lax.broadcasted_iota(jnp.int32, (PAIR, tokens), 0)
+    group = lax.shift_right_logical(slots, SLOTS.bit_length() - 1)
+    to_dest = lax.broadcasted_iota(jnp.int32, (CTX, tokens), 0) == dest
+    to_dest = jnp.where(to_dest, 1.0, 0.0).astype(BF16)
+    equal = jnp.where(near == group, 1.0, 0.0).astype(BF16)
+    less = jnp.where(near < group, 1.0, 0.0).astype(BF16)
+    dims = (((1,), (1,)), ((), ()))
+    count = lax.dot_general(to_dest, equal, dims, preferred_element_type=F32)
+    start = lax.dot_general(to_dest, less, dims, preferred_element_type=F32)
+    start_down = lax.dot_general(less, to_dest, dims, preferred_element_type=F32)
+    first = jnp.dot(start_down.astype(BF16), to_dest, preferred_element_type=F32)
+    first = jnp.sum(jnp.where(slots == near * SLOTS, first, 0.0), axis=0, keepdims=True)
+    at = first.astype(jnp.int32) + rank
+    code_ref[...] = dest * PAIR + at
+    slot = lax.broadcasted_iota(jnp.int32, (CTX, PAIR), 1) & (SLOTS - 1)
+    slot = slot.astype(F32)
+    slot_rows[...] = jnp.where(slot < count, start + slot, NO_ROW)
+    most = jnp.max(start + count, axis=0, keepdims=True)
+    most = jnp.max(most, axis=1, keepdims=True)
+    over = jnp.where(most > ROOM, 1.0, 0.0)
+    index = lax.broadcasted_iota(jnp.int32, (ROOM, tokens), 0)
+    row_hot[...] = jnp.where(index == at, 1.0, 0.0).astype(BF16)
+    inside = []
+    for column in down:
+        parts = [
+            (column >= f * fold * LOCAL) & (column < (f + 1) * fold * LOCAL)
+            for f in range(folds)
         ]
-        for copy in copies:
-            copy.start()
-        ids = ids_ref[...]
-        rank, down = ranks_of(ids)
-        dest, near = ids // LOCAL, ids % LOCAL
-        dest_ref[...] = dest
-        slots = lax.broadcasted_iota(jnp.int32, (PAIR, tokens), 0)
-        group = slots // SLOTS
-        to_dest = lax.broadcasted_iota(jnp.int32, (CTX, tokens), 0) == dest
-        to_dest = jnp.where(to_dest, 1.0, 0.0).astype(BF16)
-        equal = jnp.where(near == group, 1.0, 0.0).astype(BF16)
-        less = jnp.where(near < group, 1.0, 0.0).astype(BF16)
-        dims = (((1,), (1,)), ((), ()))
-        count = lax.dot_general(to_dest, equal, dims, preferred_element_type=F32)
-        start = lax.dot_general(to_dest, less, dims, preferred_element_type=F32)
-        start_down = lax.dot_general(less, to_dest, dims, preferred_element_type=F32)
-        first = jnp.dot(start_down.astype(BF16), to_dest, preferred_element_type=F32)
-        first = jnp.sum(jnp.where(slots == near * SLOTS, first, 0.0), axis=0, keepdims=True)
-        at = first.astype(jnp.int32) + rank
-        at_ref[...] = at
-        slot = lax.broadcasted_iota(jnp.int32, (CTX, PAIR), 1) % SLOTS
-        slot = slot.astype(F32)
-        slot_rows[...] = jnp.where(slot < count, start + slot, NO_ROW)
-        most = jnp.max(start + count, axis=0, keepdims=True)
-        most = jnp.max(most, axis=1, keepdims=True)
-        over[...] = jnp.broadcast_to(jnp.where(most > ROOM, 1.0, 0.0), over.shape)
-        index = lax.broadcasted_iota(jnp.int32, (ROOM, tokens), 0)
-        row_hot[...] = jnp.where(index == at, 1.0, 0.0).astype(BF16)
-        inside = []
-        for column in down:
-            parts = [
-                (column >= f * fold * LOCAL) & (column < (f + 1) * fold * LOCAL)
-                for f in range(folds)
-            ]
-            inside.append([jnp.where(part, 1.0, 0.0).astype(BF16) for part in parts])
-        for i, copy in enumerate(copies):
-            copy.wait()
-            for j, parts in enumerate(inside):
-                block = held[i, j * TILE : (j + 1) * TILE, :]
-                for f, part in enumerate(parts):
-                    low = (3 * f + i) * HD
-                    rows[j * TILE : (j + 1) * TILE, low : low + HD] = block * part
-
-    for i in range(per_step):
-        mine = jnp.where(dest_ref[...] % fold == step * per_step + i, 1.0, 0.0)
-        mine = jnp.broadcast_to(mine, (16, tokens)).astype(BF16)
-        here = row_hot[...].reshape(ROOM // 16, 16, tokens) * mine[None]
-        hot[i * ROOM : (i + 1) * ROOM, :] = here.reshape(ROOM, tokens)
-    placed = jnp.dot(hot[...], rows[...], preferred_element_type=F32).astype(BF16)
+        inside.append([jnp.where(part, 1.0, 0.0).astype(BF16) for part in parts])
+    for i, copy in enumerate(copies):
+        copy.wait()
+        for j, parts in enumerate(inside):
+            block = held[i, j * TILE : (j + 1) * TILE, :]
+            for f, part in enumerate(parts):
+                low = (3 * f + i) * HD
+                rows[j * TILE : (j + 1) * TILE, low : low + HD] = block * part
+
+    near_dest = dest & (fold - 1)
     line = lax.broadcasted_iota(jnp.int32, (META, HD), 0)
-    for f in range(folds):
-        for part in range(3):
-            low = (3 * f + part) * HD
-            columns = placed[:, low : low + HD].reshape(per_step, ROOM, HD)
-            out_ref[f, :, part * ROOM : (part + 1) * ROOM] = columns
+    leaving = []
+    for step in range(fold // per_step):
+        these = slice(step * per_step, (step + 1) * per_step)
         for i in range(per_step):
-            mine = slot_rows[pl.ds(f * fold + step * per_step + i, 1), :]
-            meta = jnp.where(line == 0, mine, jnp.where(line == 1, over[...], 0.0))
-            out_ref[f, i, 3 * ROOM :] = meta.astype(BF16)
-
-
-def pack(ids_row, queries, keys, values, per_step=8, folds=2):
+            mine = jnp.where(near_dest == step * per_step + i, 1.0, 0.0)
+            mine = jnp.broadcast_to(mine, (16, tokens)).astype(BF16)
+            here = row_hot[...].reshape(ROOM // 16, 16, tokens) * mine[None]
+            hot[i * ROOM : (i + 1) * ROOM, :] = here.reshape(ROOM, tokens)
+        placed = jnp.dot(hot[...], rows[...], preferred_element_type=F32).astype(BF16)
+        for f in range(folds):
+            for part in range(3):
+                low = (3 * f + part) * HD
+                columns = placed[:, low : low + HD].reshape(per_step, ROOM, HD)
+                out_ref[f, these, part * ROOM : (part + 1) * ROOM] = columns
+            for i in range(step * per_step, (step + 1) * per_step):
+                mine = slot_rows[f * fold + i : f * fold + i + 1, :]
+                meta = jnp.where(line == 0, mine, jnp.where(line == 1, over, 0.0))
+                out_ref[f, i, 3 * ROOM :] = meta.astype(BF16)
+            there = pl.ds(step * per_step, per_step)
+            leaving.append(
+                pltpu.make_async_copy(
+                    out_ref.at[f, there], sent_ref.at[f, there], gone.at[f, step]
+                )
+            )
+            leaving[-1].start()
+    for copy in leaving:
+        copy.wait()
+
+
+def pack(ids_row, queries, keys, values, per_step=4, folds=2):
     tokens = queries.shape[0]
-    line = pl.BlockSpec((1, tokens), lambda s: (0, 0))
-    anywhere = pl.BlockSpec(memory_space=pl.ANY)
-    outgoing, dest, at = pl.pallas_call(
+    vmem = pl.BlockSpec(memory_space=pltpu.VMEM)
+    hbm = pl.BlockSpec(memory_space=pltpu.HBM)
+    outgoing, code = pl.pallas_call(
         pack_kernel,
-        grid=(CTX // folds // per_step,),
         out_shape=(
             jax.ShapeDtypeStruct((folds, CTX // folds, CHUNK, HD), BF16),
             jax.ShapeDtypeStruct((1, tokens), jnp.int32),
-            jax.ShapeDtypeStruct((1, tokens), jnp.int32),
-        ),
-        in_specs=[line, anywhere, anywhere, anywhere],
-        out_specs=(
-            pl.BlockSpec((folds, per_step, CHUNK, HD), lambda s: (0, s, 0, 0)),
-            line,
-            line,
-        ),
+        ),
+        in_specs=[vmem, hbm, hbm, hbm],
+        out_specs=(hbm, vmem),
         scratch_shapes=[
             pltpu.VMEM((3, tokens, HD), BF16),
             pltpu.VMEM((tokens, 3 * folds * HD), BF16),
             pltpu.VMEM((ROOM, tokens), BF16),
             pltpu.VMEM((per_step * ROOM, tokens), BF16),
             pltpu.VMEM((CTX, PAIR), F32),
-            pltpu.VMEM((META, HD), F32),
+            pltpu.VMEM((folds, CTX // folds, CHUNK, HD), BF16),
             pltpu.SemaphoreType.DMA((3,)),
+            pltpu.SemaphoreType.DMA((folds, CTX // folds // per_step)),
         ],
-        compiler_params=pltpu.CompilerParams(
-            dimension_semantics=("arbitrary",), vmem_limit_bytes=60 << 20
-        ),
+        compiler_params=pltpu.CompilerParams(vmem_limit_bytes=60 << 20),
         cost_estimate=pl.CostEstimate(
             flops=2 * CTX * ROOM * tokens * 3 * HD, bytes_accessed=5 << 20, transcendentals=0
         ),
         name="pack",
     )(ids_row, queries, keys, values)
-    return outgoing.reshape(CTX, CHUNK, HD), dest, at
+    return outgoing.reshape(CTX, CHUNK, HD), code
 
 
 def mix_kernel(recv_ref, old_ref, out_ref, sums_ref, over_ref, wide, mixed, total):
@@ -431,43 +432,43 @@
     )(recv, old_sums)
 
 
-def unpack_kernel(dest_ref, at_ref, back_ref, out_ref, table):
+def unpack_kernel(code_ref, back_ref, out_ref, table):
     tokens = out_ref.shape[0]
+    groups = table.shape[0] // PAIR
 
     @pl.when(pl.program_id(0) == 0)
     def _():
         for i in range(CTX):
-            low, high = (i % 8) * PAIR, i // 8 * HD
+            low, high = (i % groups) * PAIR, i // groups * HD
             table[low : low + ROOM, high : high + HD] = back_ref[i]
             table[low + ROOM : low + PAIR, high : high + HD] = jnp.zeros((PAIR - ROOM, HD), BF16)
 
     lanes = lax.broadcasted_iota(jnp.int32, (TILE, PAIR), 1)
-
-    def down(ref, j):
-        here = ref[:, j * TILE : (j + 1) * TILE].astype(F32)
-        return jnp.transpose(jnp.broadcast_to(here, (TILE, TILE))).astype(jnp.int32)
-
     for j in range(tokens // TILE):
-        dest = down(dest_ref, j)
-        slot = jnp.where(lanes == down(at_ref, j), 1.0, 0.0)
-        hot = [jnp.where(dest % 8 == i, slot, 0.0).astype(BF16) for i in range(8)]
+        here = code_ref[:, j * TILE : (j + 1) * TILE].astype(F32)
+        down = jnp.transpose(jnp.broadcast_to(here, (TILE, TILE))).astype(jnp.int32)
+        inner = down & (groups * PAIR - 1)
+        outer = lax.shift_right_logical(down, (groups * PAIR).bit_length() - 1)
+        hot = [jnp.where(inner == lanes + i * PAIR, 1.0, 0.0).astype(BF16) for i in range(groups)]
         found = jnp.dot(jnp.concatenate(hot, axis=1), table[...], preferred_element_type=F32)
         row = found[:, 0:HD]
-        for i in range(1, CTX // 8):
-            row = jnp.where(dest // 8 == i, found[:, i * HD : (i + 1) * HD], row)
+        for i in range(1, CTX // groups):
+            row = jnp.where(outer == i, found[:, i * HD : (i + 1) * HD], row)
         out_ref[j * TILE : (j + 1) * TILE, :] = row.astype(BF16)
 
 
-def unpack(dest, at, back, tile=1024):
-    tokens = dest.shape[1]
-    line = pl.BlockSpec((1, tile), lambda s: (0, s))
+def unpack(code, back, tile=2048, groups=8):
+    tokens = code.shape[1]
     return pl.pallas_call(
         unpack_kernel,
         grid=(tokens // tile,),
         out_shape=jax.ShapeDtypeStruct((tokens, HD), BF16),
-        in_specs=[line, line, pl.BlockSpec((CTX, ROOM, HD), lambda s: (0, 0, 0))],
+        in_specs=[
+            pl.BlockSpec((1, tile), lambda s: (0, s)),
+            pl.BlockSpec((CTX, ROOM, HD), lambda s: (0, 0, 0)),
+        ],
         out_specs=pl.BlockSpec((tile, HD), lambda s: (s, 0)),
-        scratch_shapes=[pltpu.VMEM((8 * PAIR, CTX // 8 * HD), BF16)],
+        scratch_shapes=[pltpu.VMEM((groups * PAIR, CTX // groups * HD), BF16)],
         compiler_params=pltpu.CompilerParams(
             dimension_semantics=("arbitrary",), vmem_limit_bytes=32 << 20
         ),
@@ -475,41 +476,95 @@
             flops=2 * tokens * 1024 * 512, bytes_accessed=2 << 20, transcendentals=0
         ),
         name="unpack",
-    )(dest, at, back)
-
-
-def project_kernel(heads_ref, w_ref, out_ref, *, columns):
-    halves, blocks = w_ref.shape[0], w_ref.shape[1]
+    )(code, back)
+
+
+def hold_kernel(w_ref, out_ref, done):
+    count = out_ref.shape[1]
+    copies = [
+        pltpu.make_async_copy(w_ref.at[c, pl.ds(0, count)], out_ref.at[c], done.at[c])
+        for c in range(w_ref.shape[0])
+    ]
+    for copy in copies:
+        copy.start()
+    for copy in copies:
+        copy.wait()
+
+
+def hold(w_all, count=KEPT):
+    halves, _, depth, width = w_all.shape
+    return pl.pallas_call(
+        hold_kernel,
+        out_shape=jax.ShapeDtypeStruct((halves, count, depth, width), w_all.dtype),
+        in_specs=[pl.BlockSpec(memory_space=pltpu.HBM)],
+        out_specs=pl.BlockSpec(memory_space=pltpu.VMEM),
+        scratch_shapes=[pltpu.SemaphoreType.DMA((halves,))],
+        compiler_params=pltpu.CompilerParams(vmem_limit_bytes=8 << 20),
+        cost_estimate=pl.CostEstimate(flops=0, bytes_accessed=16 << 20, transcendentals=0),
+        name="hold",
+    )(w_all)
+
+
+def project_kernel(heads_ref, kept_ref, w_ref, out_ref, held, done):
+    halves, steps, columns = held.shape[1], held.shape[0], held.shape[2]
+    first = kept_ref.shape[1]
     each = heads_ref.shape[0] // halves
+    copies = [
+        [
+            pltpu.make_async_copy(
+                w_ref.at[c, pl.ds(first + p * columns, columns)], held.at[p, c], done.at[p, c]
+            )
+            for c in range(halves)
+        ]
+        for p in range(steps)
+    ]
+    for pair in copies:
+        for copy in pair:
+            copy.start()
     left = [
         jnp.concatenate([heads_ref[c * each + i] for i in range(each)], axis=1)
         for c in range(halves)
     ]
-    for low in range(0, blocks, columns):
+
+    def multiply(parts, low):
         total = 0.0
-        for c in range(halves):
-            right = jnp.concatenate([w_ref[c, low + n] for n in range(columns)], axis=1)
+        for c, blocks in enumerate(parts):
+            right = jnp.concatenate(blocks, axis=1)
             total = total + jnp.dot(left[c], right, preferred_element_type=F32)
-        for n in range(columns):
+        for n in range(len(parts[0])):
             out_ref[low + n] = total[:, n * HD : (n + 1) * HD].astype(BF16)
 
-
-def project(heads, w_all, columns=4):
+    multiply([[kept_ref[c, n] for n in range(first)] for c in range(halves)], 0)
+    for p, pair in enumerate(copies):
+        for copy in pair:
+            copy.wait()
+        multiply(
+            [[held[p, c, n] for n in range(columns)] for c in range(halves)], first + p * columns
+        )
+
+
+def project(heads, kept, w_all, columns=4):
     halves, blocks, depth, width = w_all.shape
     tokens = heads.shape[1]
+    steps = (blocks - kept.shape[1]) // columns
+    vmem = pl.BlockSpec(memory_space=pltpu.VMEM)
     return pl.pallas_call(
-        functools.partial(project_kernel, columns=columns),
+        project_kernel,
         out_shape=jax.ShapeDtypeStruct((blocks, tokens, width), BF16),
-        in_specs=[pl.BlockSpec(memory_space=pltpu.VMEM)] * 2,
-        out_specs=pl.BlockSpec(memory_space=pltpu.VMEM),
-        compiler_params=pltpu.CompilerParams(vmem_limit_bytes=32 << 20),
+        in_specs=[vmem, vmem, pl.BlockSpec(memory_space=pltpu.HBM)],
+        out_specs=vmem,
+        scratch_shapes=[
+            pltpu.VMEM((steps, halves, columns, depth, width), BF16),
+            pltpu.SemaphoreType.DMA((steps, halves)),
+        ],
+        compiler_params=pltpu.CompilerParams(vmem_limit_bytes=48 << 20),
         cost_estimate=pl.CostEstimate(
             flops=2 * tokens * halves * depth * blocks * width,
             bytes_accessed=9 << 20,
             transcendentals=0,
         ),
         name="project",
-    )(heads, w_all)
+    )(heads, kept, w_all)
 
 
 def over_ctx(chunks):
@@ -522,13 +577,13 @@
     half = w_out.shape[0] // 2
     w_half = lax.dynamic_slice_in_dim(w_out, lax.axis_index("ctx") % 2 * half, half)
     ids_row = cluster_ids[:, :, 0]
-    outgoing, dest, at = pack(ids_row, queries, keys, values)
+    outgoing, code = pack(ids_row, queries, keys, values)
     chips = [list(range(2 * hg_count * i, 2 * hg_count * (i + 1))) for i in range(CTX // 2)]
     w_all = lax.all_gather(w_half, ("ctx", "hg"), axis_index_groups=chips)
     mixed_rows, sums, over = mix(over_ctx(outgoing), old_sums[0])
 
     def compact():
-        return unpack(dest, at, over_ctx(mixed_rows)), sums
+        return unpack(code, over_ctx(mixed_rows)), sums
 
     def general():
         slots, target = place(ids_row, queries, keys, values)
@@ -539,7 +594,7 @@
     attention = attention.reshape(hg_count, tok_rows // hg_count, HD)
     all_heads = lax.all_to_all(attention, "hg", split_axis=0, concat_axis=0, tiled=True)
     w_all = w_all.reshape(2, hg_count, -1, w_out.shape[1])
-    mixed = project(all_heads, w_all)
+    mixed = project(all_heads, hold(w_all), w_all)
     projected = lax.all_to_all(mixed, "hg", split_axis=0, concat_axis=0, tiled=True)
     return (projected.reshape(tok_rows, w_out.shape[1]), centroid_sums[None])
 

time: 180 us -> 178 us (0.989)
  blocking collectives: 96.2 us -> 54 us
  waiting for transfers between devices: 31.7 us -> 57.5 us
  starting transfers between devices: 9.81 us -> 22.9 us
  Pallas kernels: 20.8 us -> 22.6 us
    all_to_all x1 -> x0, blocking collectives: 42.2 us -> none  [on_device(): lax.all_to_all(attention, 'hg', split_axis=0, concat_axis=0, tiled=True)]
    all_to_all x0 -> x1, waiting for transfers between devices: none -> 25.7 us  [on_device(): lax.all_to_all(attention, 'hg', split_axis=0, concat_axis=0, tiled=True)]
    all_to_all x0 -> x1, starting transfers between devices: none -> 13.1 us  [on_device(): lax.all_to_all(attention, 'hg', split_axis=0, concat_axis=0, tiled=True)]
    pallas_call x2 -> x3, Pallas kernels: 10.8 us -> 12.6 us  [the longest x1 9.09 us: pack(): pl.pallas_call(pack_kernel, out_shape=(jax.ShapeDtypeStruct((folds, CTX /...]
  transfers between devices with their start and end apart: 2 -> 3, of which waited for: 1 -> 2; matrix products, arithmetic and copies ran while one was open for 0% -> 0% of each run, Pallas kernels for 11% -> 11%
where the time goes in v5:
time: 178 us
  waiting for transfers between devices  57.5 us (32%)
  blocking collectives  54 us (30%)
  starting transfers between devices  22.9 us (13%)
  Pallas kernels  22.6 us (13%)
  between operations  14.8 us (8%)
  local copies, waits for them, and re-layouts  5.89 us (3%)
    all_to_all x1, blocking collectives, on_device(): lax.all_to_all(mixed, 'hg', split_axis=0, concat_axis=0, tiled=True)  35.5 us
    all_to_all x1, waiting for transfers between devices, over_ctx(): lax.all_to_all(chunks, 'ctx', split_axis=0, concat_axis=0, tiled=True)  31.7 us
    all_to_all x1, waiting for transfers between devices, on_device(): lax.all_to_all(attention, 'hg', split_axis=0, concat_axis=0, tiled=True)  25.7 us
    all_to_all x1, blocking collectives, over_ctx(): lax.all_to_all(chunks, 'ctx', split_axis=0, concat_axis=0, tiled=True)  18.5 us
    all_to_all x1, starting transfers between devices, on_device(): lax.all_to_all(attention, 'hg', split_axis=0, concat_axis=0, tiled=True)  13.1 us
    all_to_all x1, starting transfers between devices, over_ctx(): lax.all_to_all(chunks, 'ctx', split_axis=0, concat_axis=0, tiled=True)  9.78 us
    pallas_call x1, Pallas kernels, pack(): pl.pallas_call(pack_kernel, out_shape=(jax.ShapeDtypeStruct((folds, CTX /...  9.09 us
    pallas_call x1, Pallas kernels, mix(): pl.pallas_call(mix_kernel, out_shape=(jax.ShapeDtypeStruct((CTX, ROOM, HD...  6.81 us
  transfers between devices with their start and end apart: 3, of which 2 were waited for; matrix products, arithmetic and copies ran while one was open for 0% of the time, Pallas kernels for 11%

profile of v5, /device:TPU:2, one launch (start us, length us, event | category | flops | bytes accessed | tf_op | source)
XLA Modules:
  0.0 177.7 jit_solution(4479031860620869551)
XLA Ops:
  7.2 0.0 copy-start
  7.2 0.0 all-gather.3.cloned.1.call-start
  7.2 1.0 copy-done
  8.2 0.7 constant_dynamic-slice_fusion
  8.9 0.0 all-gather.3.cloned.1.call-update
  9.0 9.1 %pack.1 = (bf16[2,16,296,128]{3,2,1,0:T(8,128)(2,1)}, s32[1,2048]{1,0:T(1,128)S(1)}) custom-call(s32[1,2048]{1,0:T(1,128)} %bitcast.15, bf16[2048,128]{1,0:T(8,128)(2,1)} %q_ref.1, bf16[2048,128]{1,0:T(8,128)(2,1)} %k_ref.1, bf16[2048,128]{1,0:T(8,128)(2,1)} %v_ref.1), custom_call_target="tpu_custom_call" | custom-call | flops 4831838208 | bytes 5242880 | tf_op jit(solution)/shard_map/pack/pallas_call | solution.py:319
  18.1 0.0 copy-start.3
  18.1 0.0 copy-start.4
  18.1 0.0 copy-start.5
  18.1 9.8 %all-to-all-start.3 = ((bf16[32,296,128]{2,1,0:T(8,128)(2,1)}), bf16[32,296,128]{2,1,0:T(8,128)(2,1)S(1)}, u32[]{:S(2)}, u32[]{:S(2)}) async-start(bf16[32,296,128]{2,1,0:T(8,128)(2,1)} %bitcast.11), calls=%async_computation.3 | async-start | bytes 4849664 | tf_op jit(solution)/shard_map/all_to_all | solution.py:571
  27.9 31.7 %all-to-all-done.3.recv_ref = bf16[32,296,128]{2,1,0:T(8,128)(2,1)S(1)} async-done(((bf16[32,296,128]{2,1,0:T(8,128)(2,1)}), bf16[32,296,128]{2,1,0:T(8,128)(2,1)S(1)}, u32[]{:S(2)}, u32[]{:S(2)}) %all-to-all-start.3) | async-done | bytes 2424864 | tf_op jit(solution)/shard_map/all_to_all | solution.py:571
  59.6 0.0 copy-done.3
  59.6 6.8 %mix.1 = (bf16[32,96,128]{2,1,0:T(8,128)(2,1)S(1)}, f32[16,128]{1,0:T(8,128)}, s32[1,1]{1,0:T(1,128)}) custom-call(bf16[32,296,128]{2,1,0:T(8,128)(2,1)S(1)} %all-to-all-done.3.recv_ref, f32[16,128]{1,0:T(8,128)S(1)} %bitcast.13), custom_call_target="tpu_custom_call" | custom-call | flops 536870912 | bytes 5242880 | tf_op jit(solution)/shard_map/mix/pallas_call | solution.py:407
  67.1 0.0 copy-done.4
  67.1 0.0 copy-done.5
  67.1 21.8 %conditional.1 = (bf16[2048,128]{1,0:T(8,128)(2,1)}, f32[16,128]{1,0:T(8,128)}) conditional(s32[]{:T(128)} %bitcast.4, (bf16[32,96,128]{2,1,0:T(8,128)(2,1)S(1)}, s32[1,2048]{1,0:T(1,128)S(1)}, f32[16,128]{1,0:T(8,128)}) %tuple.16, (s32[1,2048]{1,0:T(1,128)S(1)}, bf16[2048,128]{1,0:T(8,128)(2,1)S(1)}, bf16[2048,128]{1,0:T(8,128)(2,1)}, ...), branch_computations={%region_0.1_spmd, %region_1.2_spmd} | conditional | flops 11274289152 | bytes 21004332 | solution.py:593
  67.1 18.5 %all_to_all.27.back_ref = bf16[32,96,128]{2,1,0:T(8,128)(2,1)S(1)} all-to-all(bf16[32,96,128]{2,1,0:T(8,128)(2,1)S(1)} %get-tuple-element.17), channel_id=1, replica_groups=mesh['ctx'=32,'hg'=16] {'ctx'}, dimensions={0} | all-to-all | bytes 1572864 | tf_op jit(solution)/shard_map/cond/branch_0_fun/all_to_all | solution.py:571
  85.6 3.3 %unpack.1 = bf16[2048,128]{1,0:T(8,128)(2,1)} custom-call(s32[1,2048]{1,0:T(1,128)S(1)} %get-tuple-element.16.code_ref, bf16[32,96,128]{2,1,0:T(8,128)(2,1)S(1)} %all_to_all.27.back_ref), custom_call_target="tpu_custom_call" | custom-call | flops 2147483648 | bytes 2097152 | tf_op jit(solution)/shard_map/cond/branch_0_fun/unpack/pallas_call | solution.py:462
  88.9 13.1 %all-to-all-start.4 = ((bf16[16,128,128]{2,1,0:T(8,128)(2,1)}), bf16[16,128,128]{2,1,0:T(8,128)(2,1)S(1)}, u32[]{:S(2)}, u32[]{:S(2)}) async-start(bf16[16,128,128]{2,1,0:T(8,128)(2,1)} %bitcast.5), calls=%async_computation.4 | async-start | bytes 1048576 | tf_op jit(solution)/shard_map/all_to_all | solution.py:595
  101.9 0.0 all-gather.3.cloned.1.call-done
  102.0 0.0 copy-start.1
  102.0 3.4 %copy-done.1 = bf16[32768,128]{1,0:T(8,128)(2,1)S(1)} copy-done((bf16[32768,128]{1,0:T(8,128)(2,1)S(1)}, bf16[32768,128]{1,0:T(8,128)(2,1)}, u32[]{:S(2)}) %copy-start.1) | copy-done | bytes 8388632
  105.4 0.2 hold.1.kept_ref
  105.5 25.7 %all-to-all-done.4.heads_ref = bf16[16,128,128]{2,1,0:T(8,128)(2,1)S(1)} async-done(((bf16[16,128,128]{2,1,0:T(8,128)(2,1)}), bf16[16,128,128]{2,1,0:T(8,128)(2,1)S(1)}, u32[]{:S(2)}, u32[]{:S(2)}) %all-to-all-start.4) | async-done | bytes 524320 | tf_op jit(solution)/shard_map/all_to_all | solution.py:595
  131.2 3.3 %project.1 = bf16[16,128,128]{2,1,0:T(8,128)(2,1)S(1)} custom-call(bf16[16,128,128]{2,1,0:T(8,128)(2,1)S(1)} %all-to-all-done.4.heads_ref, bf16[2,4,1024,128]{3,2,1,0:T(8,128)(2,1)S(1)} %hold.1.kept_ref, bf16[2,16,1024,128]{3,2,1,0:T(8,128)(2,1)} %bitcast.9), custom_call_target="tpu_custom_call" | custom-call | flops 1073741824 | bytes 9437184 | tf_op jit(solution)/shard_map/project/pallas_call | solution.py:551
  134.5 35.5 %all_to_all.30 = bf16[16,128,128]{2,1,0:T(8,128)(2,1)S(1)} all-to-all(bf16[16,128,128]{2,1,0:T(8,128)(2,1)S(1)} %project.1), channel_id=1, replica_groups=mesh['ctx'=32,'hg'=16] {'hg'}, dimensions={0} | all-to-all | bytes 1048576 | tf_op jit(solution)/shard_map/all_to_all | solution.py:598
  170.1 0.8 copy.13
Async XLA Ops:
  7.2 1.0 copy-start
  7.2 94.8 %all-gather.3.cloned.1.call-start = ((), (), s32[]{:S(2)}) async-start(), calls=%async_computation.6 | async-start | bytes 8650752 | tf_op jit(solution)/shard_map/all_gather | solution.py:582
  18.1 41.5 %copy-start.3 = (f32[1,16,128]{2,1,0:T(8,128)S(1)}, f32[1,16,128]{2,1,0:T(8,128)}, u32[]{:S(2)}) copy-start(f32[1,16,128]{2,1,0:T(8,128)} %param.13) | copy-start | bytes 24580
  18.1 49.0 %copy-start.4 = (bf16[2048,128]{1,0:T(8,128)(2,1)S(1)}, bf16[2048,128]{1,0:T(8,128)(2,1)}, u32[]{:S(2)}) copy-start(bf16[2048,128]{1,0:T(8,128)(2,1)} %q_ref.1) | copy-start | bytes 1572868
  18.1 49.0 %copy-start.5 = (s32[1,2048,1]{1,2,0:T(1,128)S(1)}, s32[1,2048,1]{1,2,0:T(1,128)}, u32[]{:S(2)}) copy-start(s32[1,2048,1]{1,2,0:T(1,128)} %param.11) | copy-start | bytes 24580
  18.1 41.5 %all-to-all-start.3 = ((bf16[32,296,128]{2,1,0:T(8,128)(2,1)}), bf16[32,296,128]{2,1,0:T(8,128)(2,1)S(1)}, u32[]{:S(2)}, u32[]{:S(2)}) async-start(bf16[32,296,128]{2,1,0:T(8,128)(2,1)} %bitcast.11), calls=%async_computation.3 | async-start | bytes 4849664 | tf_op jit(solution)/shard_map/all_to_all | solution.py:571
  88.9 42.4 %all-to-all-start.4 = ((bf16[16,128,128]{2,1,0:T(8,128)(2,1)}), bf16[16,128,128]{2,1,0:T(8,128)(2,1)S(1)}, u32[]{:S(2)}, u32[]{:S(2)}) async-start(bf16[16,128,128]{2,1,0:T(8,128)(2,1)} %bitcast.5), calls=%async_computation.4 | async-start | bytes 1048576 | tf_op jit(solution)/shard_map/all_to_all | solution.py:595
  102.0 3.4 %copy-start.1 = (bf16[32768,128]{1,0:T(8,128)(2,1)S(1)}, bf16[32768,128]{1,0:T(8,128)(2,1)}, u32[]{:S(2)}) copy-start(bf16[32768,128]{1,0:T(8,128)(2,1)} %all-gather.3.cloned.1.call-done) | copy-start | bytes 25165828
Sparse Core Ops, SparseCore 0:
  10.1 83.8 all-gather.2

commit v6 on v5

--- a/solution.py
+++ b/solution.py
@@ -590,7 +590,7 @@
         slot_rows, slot_sums = attend(over_ctx(slots), old_sums[0])
         return fetch(target, over_ctx(slot_rows)), slot_sums
 
-    attention, centroid_sums = lax.cond(over[0, 0] > 0, general, compact)
+    attention, centroid_sums = lax.switch(over[0, 0], [compact, general])
     attention = attention.reshape(hg_count, tok_rows // hg_count, HD)
     all_heads = lax.all_to_all(attention, "hg", split_axis=0, concat_axis=0, tiled=True)
     w_all = w_all.reshape(2, hg_count, -1, w_out.shape[1])

time: 178 us -> 178 us (level)
  no operation moved by 1% of the time
where the time goes in v6:
time: 178 us
  waiting for transfers between devices  57.5 us (32%)
  blocking collectives  54 us (30%)
  starting transfers between devices  22.9 us (13%)
  Pallas kernels  22.6 us (13%)
  between operations  14.8 us (8%)
  local copies, waits for them, and re-layouts  5.89 us (3%)
    all_to_all x1, blocking collectives, on_device(): lax.all_to_all(mixed, 'hg', split_axis=0, concat_axis=0, tiled=True)  35.5 us
    all_to_all x1, waiting for transfers between devices, over_ctx(): lax.all_to_all(chunks, 'ctx', split_axis=0, concat_axis=0, tiled=True)  31.7 us
    all_to_all x1, waiting for transfers between devices, on_device(): lax.all_to_all(attention, 'hg', split_axis=0, concat_axis=0, tiled=True)  25.7 us
    all_to_all x1, blocking collectives, over_ctx(): lax.all_to_all(chunks, 'ctx', split_axis=0, concat_axis=0, tiled=True)  18.5 us
    all_to_all x1, starting transfers between devices, on_device(): lax.all_to_all(attention, 'hg', split_axis=0, concat_axis=0, tiled=True)  13.1 us
    all_to_all x1, starting transfers between devices, over_ctx(): lax.all_to_all(chunks, 'ctx', split_axis=0, concat_axis=0, tiled=True)  9.78 us
    pallas_call x1, Pallas kernels, pack(): pl.pallas_call(pack_kernel, out_shape=(jax.ShapeDtypeStruct((folds, CTX /...  9.09 us
    pallas_call x1, Pallas kernels, mix(): pl.pallas_call(mix_kernel, out_shape=(jax.ShapeDtypeStruct((CTX, ROOM, HD...  6.81 us
  transfers between devices with their start and end apart: 3, of which 2 were waited for; matrix products, arithmetic and copies ran while one was open for 0% of the time, Pallas kernels for 11%

profile of v6, /device:TPU:2, one launch (start us, length us, event | category | flops | bytes accessed | tf_op | source)
XLA Modules:
  0.0 177.7 jit_solution(18022228495494401812)
XLA Ops:
  7.2 0.0 copy-start
  7.2 0.0 all-gather.3.cloned.1.call-start
  7.2 1.0 copy-done
  8.2 0.7 constant_dynamic-slice_fusion
  8.9 0.0 all-gather.3.cloned.1.call-update
  9.0 9.1 %pack.1 = (bf16[2,16,296,128]{3,2,1,0:T(8,128)(2,1)}, s32[1,2048]{1,0:T(1,128)S(1)}) custom-call(s32[1,2048]{1,0:T(1,128)} %bitcast.15, bf16[2048,128]{1,0:T(8,128)(2,1)} %q_ref.1, bf16[2048,128]{1,0:T(8,128)(2,1)} %k_ref.1, bf16[2048,128]{1,0:T(8,128)(2,1)} %v_ref.1), custom_call_target="tpu_custom_call" | custom-call | flops 4831838208 | bytes 5242880 | tf_op jit(solution)/shard_map/pack/pallas_call | solution.py:319
  18.1 0.0 copy-start.3
  18.1 0.0 copy-start.4
  18.1 0.0 copy-start.5
  18.1 9.8 %all-to-all-start.3 = ((bf16[32,296,128]{2,1,0:T(8,128)(2,1)}), bf16[32,296,128]{2,1,0:T(8,128)(2,1)S(1)}, u32[]{:S(2)}, u32[]{:S(2)}) async-start(bf16[32,296,128]{2,1,0:T(8,128)(2,1)} %bitcast.11), calls=%async_computation.3 | async-start | bytes 4849664 | tf_op jit(solution)/shard_map/all_to_all | solution.py:571
  27.9 31.7 %all-to-all-done.3.recv_ref = bf16[32,296,128]{2,1,0:T(8,128)(2,1)S(1)} async-done(((bf16[32,296,128]{2,1,0:T(8,128)(2,1)}), bf16[32,296,128]{2,1,0:T(8,128)(2,1)S(1)}, u32[]{:S(2)}, u32[]{:S(2)}) %all-to-all-start.3) | async-done | bytes 2424864 | tf_op jit(solution)/shard_map/all_to_all | solution.py:571
  59.6 0.0 copy-done.3
  59.6 6.8 %mix.1 = (bf16[32,96,128]{2,1,0:T(8,128)(2,1)S(1)}, f32[16,128]{1,0:T(8,128)}, s32[1,1]{1,0:T(1,128)}) custom-call(bf16[32,296,128]{2,1,0:T(8,128)(2,1)S(1)} %all-to-all-done.3.recv_ref, f32[16,128]{1,0:T(8,128)S(1)} %bitcast.13), custom_call_target="tpu_custom_call" | custom-call | flops 536870912 | bytes 5242880 | tf_op jit(solution)/shard_map/mix/pallas_call | solution.py:407
  67.1 0.0 copy-done.4
  67.1 0.0 copy-done.5
  67.1 21.8 %conditional.1 = (bf16[2048,128]{1,0:T(8,128)(2,1)}, f32[16,128]{1,0:T(8,128)}) conditional(s32[]{:T(128)} %bitcast.4, (bf16[32,96,128]{2,1,0:T(8,128)(2,1)S(1)}, s32[1,2048]{1,0:T(1,128)S(1)}, f32[16,128]{1,0:T(8,128)}) %tuple.16, (s32[1,2048]{1,0:T(1,128)S(1)}, bf16[2048,128]{1,0:T(8,128)(2,1)S(1)}, bf16[2048,128]{1,0:T(8,128)(2,1)}, ...), branch_computations={%region_0.1_spmd, %region_1.2_spmd} | conditional | flops 11274289152 | bytes 21004332 | solution.py:593
  67.1 18.5 %all_to_all.27.back_ref = bf16[32,96,128]{2,1,0:T(8,128)(2,1)S(1)} all-to-all(bf16[32,96,128]{2,1,0:T(8,128)(2,1)S(1)} %get-tuple-element.17), channel_id=1, replica_groups=mesh['ctx'=32,'hg'=16] {'ctx'}, dimensions={0} | all-to-all | bytes 1572864 | tf_op jit(solution)/shard_map/cond/branch_0_fun/all_to_all | solution.py:571
  85.6 3.3 %unpack.1 = bf16[2048,128]{1,0:T(8,128)(2,1)} custom-call(s32[1,2048]{1,0:T(1,128)S(1)} %get-tuple-element.16.code_ref, bf16[32,96,128]{2,1,0:T(8,128)(2,1)S(1)} %all_to_all.27.back_ref), custom_call_target="tpu_custom_call" | custom-call | flops 2147483648 | bytes 2097152 | tf_op jit(solution)/shard_map/cond/branch_0_fun/unpack/pallas_call | solution.py:462
  88.9 13.1 %all-to-all-start.4 = ((bf16[16,128,128]{2,1,0:T(8,128)(2,1)}), bf16[16,128,128]{2,1,0:T(8,128)(2,1)S(1)}, u32[]{:S(2)}, u32[]{:S(2)}) async-start(bf16[16,128,128]{2,1,0:T(8,128)(2,1)} %bitcast.5), calls=%async_computation.4 | async-start | bytes 1048576 | tf_op jit(solution)/shard_map/all_to_all | solution.py:595
  101.9 0.0 all-gather.3.cloned.1.call-done
  102.0 0.0 copy-start.1
  102.0 3.4 %copy-done.1 = bf16[32768,128]{1,0:T(8,128)(2,1)S(1)} copy-done((bf16[32768,128]{1,0:T(8,128)(2,1)S(1)}, bf16[32768,128]{1,0:T(8,128)(2,1)}, u32[]{:S(2)}) %copy-start.1) | copy-done | bytes 8388632
  105.4 0.2 hold.1.kept_ref
  105.5 25.7 %all-to-all-done.4.heads_ref = bf16[16,128,128]{2,1,0:T(8,128)(2,1)S(1)} async-done(((bf16[16,128,128]{2,1,0:T(8,128)(2,1)}), bf16[16,128,128]{2,1,0:T(8,128)(2,1)S(1)}, u32[]{:S(2)}, u32[]{:S(2)}) %all-to-all-start.4) | async-done | bytes 524320 | tf_op jit(solution)/shard_map/all_to_all | solution.py:595
  131.2 3.3 %project.1 = bf16[16,128,128]{2,1,0:T(8,128)(2,1)S(1)} custom-call(bf16[16,128,128]{2,1,0:T(8,128)(2,1)S(1)} %all-to-all-done.4.heads_ref, bf16[2,4,1024,128]{3,2,1,0:T(8,128)(2,1)S(1)} %hold.1.kept_ref, bf16[2,16,1024,128]{3,2,1,0:T(8,128)(2,1)} %bitcast.9), custom_call_target="tpu_custom_call" | custom-call | flops 1073741824 | bytes 9437184 | tf_op jit(solution)/shard_map/project/pallas_call | solution.py:551
  134.5 35.5 %all_to_all.30 = bf16[16,128,128]{2,1,0:T(8,128)(2,1)S(1)} all-to-all(bf16[16,128,128]{2,1,0:T(8,128)(2,1)S(1)} %project.1), channel_id=1, replica_groups=mesh['ctx'=32,'hg'=16] {'hg'}, dimensions={0} | all-to-all | bytes 1048576 | tf_op jit(solution)/shard_map/all_to_all | solution.py:598
  170.1 0.8 copy.13
Async XLA Ops:
  7.2 1.0 copy-start
  7.2 94.8 %all-gather.3.cloned.1.call-start = ((), (), s32[]{:S(2)}) async-start(), calls=%async_computation.6 | async-start | bytes 8650752 | tf_op jit(solution)/shard_map/all_gather | solution.py:582
  18.1 41.5 %copy-start.3 = (f32[1,16,128]{2,1,0:T(8,128)S(1)}, f32[1,16,128]{2,1,0:T(8,128)}, u32[]{:S(2)}) copy-start(f32[1,16,128]{2,1,0:T(8,128)} %param.13) | copy-start | bytes 24580
  18.1 49.0 %copy-start.4 = (bf16[2048,128]{1,0:T(8,128)(2,1)S(1)}, bf16[2048,128]{1,0:T(8,128)(2,1)}, u32[]{:S(2)}) copy-start(bf16[2048,128]{1,0:T(8,128)(2,1)} %q_ref.1) | copy-start | bytes 1572868
  18.1 49.0 %copy-start.5 = (s32[1,2048,1]{1,2,0:T(1,128)S(1)}, s32[1,2048,1]{1,2,0:T(1,128)}, u32[]{:S(2)}) copy-start(s32[1,2048,1]{1,2,0:T(1,128)} %param.11) | copy-start | bytes 24580
  18.1 41.5 %all-to-all-start.3 = ((bf16[32,296,128]{2,1,0:T(8,128)(2,1)}), bf16[32,296,128]{2,1,0:T(8,128)(2,1)S(1)}, u32[]{:S(2)}, u32[]{:S(2)}) async-start(bf16[32,296,128]{2,1,0:T(8,128)(2,1)} %bitcast.11), calls=%async_computation.3 | async-start | bytes 4849664 | tf_op jit(solution)/shard_map/all_to_all | solution.py:571
  88.9 42.4 %all-to-all-start.4 = ((bf16[16,128,128]{2,1,0:T(8,128)(2,1)}), bf16[16,128,128]{2,1,0:T(8,128)(2,1)S(1)}, u32[]{:S(2)}, u32[]{:S(2)}) async-start(bf16[16,128,128]{2,1,0:T(8,128)(2,1)} %bitcast.5), calls=%async_computation.4 | async-start | bytes 1048576 | tf_op jit(solution)/shard_map/all_to_all | solution.py:595
  102.0 3.4 %copy-start.1 = (bf16[32768,128]{1,0:T(8,128)(2,1)S(1)}, bf16[32768,128]{1,0:T(8,128)(2,1)}, u32[]{:S(2)}) copy-start(bf16[32768,128]{1,0:T(8,128)(2,1)} %all-gather.3.cloned.1.call-done) | copy-start | bytes 25165828
Sparse Core Ops, SparseCore 0:
  10.1 83.8 all-gather.2
